TPU v7x, 32 devices: a whole 2x2x4 slice. The times are simulated.
32 devices in a mesh: gx: 8 (over z, x), gy: 4 (over y, core).
Axes of the slice: x: 2, y: 2, z: 4, core: 2. Of those that a mesh axis runs over, the one named last changes fastest.
Arguments:
- features: bfloat16 [32768, 512], P(('gx', 'gy')), may hold values from -6 to 6
- zorder_rank: int32 [32768], P(('gx', 'gy')), may hold values from 0 to 32767, as said below
- hilbert_rank: int32 [32768], P(('gx', 'gy')), may hold values from 0 to 32767, as said below
- attention_gain: float32 [2, 512], replicated, may hold values from 0.1 to 1.9
- attention_in: bfloat16 [2, 512, 1536], replicated, may hold values from -2 to 2
- attention_out: bfloat16 [2, 512, 512], replicated, may hold values from -0.25 to 0.25
- feedforward_gain: float32 [2, 512], replicated, may hold values from 0.1 to 1.9
- feedforward_up: bfloat16 [2, 512, 2048], replicated, may hold values from -0.25 to 0.25
- feedforward_down: bfloat16 [2, 2048, 512], replicated, may hold values from -0.125 to 0.125
Outputs:
- output_rows: bfloat16 [32768, 512], P(('gx', 'gy'))
Inputs may be any that keep to these rules, and one draw needn't show every extreme that they name: `zorder_rank`: every value appears once. Device d (gx index times 4 plus gy index) owns the ranks d * 1024 to d * 1024 + 1023. Of one device's points at most 80 have ranks in one device's range, and some device sends exactly 80 into some range. `hilbert_rank`: every value appears once, with ranges owned as for zorder_rank. Of one device's points at most 80 have ranks in one device's range; of the points whose zorder_rank lies in one device's range, at most 80 have hilbert_rank in one device's range; both bounds are reached.
All inputs are finite; a program needn't handle non-finite values.
Results may differ from a plain program's by a relative error of at most 0.03.
The roundings to bfloat16 on the way count: a program that leaves them out, or rounds other values in their place, can miss the bound.
Values may be sent and summed in bfloat16 or wider, within the bound.
No kernel may reach another device: no remote copies, remote signals or barrier semaphores. Data moves between devices by JAX's collectives and lax.ppermute only.
A program may use at most 128 MiB of HBM per device.

v0:
```python
import jax
import jax.numpy as jnp
from jax import lax
from jax.sharding import PartitionSpec as P

HEADS = 32
PATCH = 1024


epsilon = 1e-05


def layer_norm(row_block, row_gain):
    values = row_block.astype(jnp.float32)
    average = jnp.mean(values, axis=-1, keepdims=True)
    centred = values - average
    variance = jnp.mean(centred * centred, axis=-1, keepdims=True)
    return (centred * lax.rsqrt(variance + epsilon) * row_gain).astype(jnp.bfloat16)


def attend(projected, heads):
    row_count, three_width = projected.shape
    model_width = three_width // 3
    head_size = model_width // heads
    groups = heads // 4
    patches = row_count // PATCH
    split = projected.reshape(patches, PATCH, 3, groups, 4, head_size).transpose(0, 3, 2, 1, 4, 5)
    split = split.reshape(patches * groups, 3, PATCH, 4, head_size)

    def one_group(part):
        scores = jnp.einsum(
            "qhd,khd->hqk", part[0], part[1], preferred_element_type=jnp.float32
        ) * head_size ** (-0.5)
        row_max = jnp.max(scores, axis=2, keepdims=True)
        raised = jnp.exp(scores - row_max)
        weights = (raised / jnp.sum(raised, axis=2, keepdims=True)).astype(jnp.bfloat16)
        return jnp.einsum(
            "hqk,khd->qhd", weights, part[2], preferred_element_type=jnp.float32
        ).astype(jnp.bfloat16)

    mixed_rows = lax.map(one_group, split)
    mixed_rows = mixed_rows.reshape(patches, groups, PATCH, 4, head_size).transpose(0, 2, 1, 3, 4)
    return mixed_rows.reshape(row_count, model_width)


def run_block(
    stream,
    layer_index,
    attention_gain,
    attention_in,
    attention_out,
    feedforward_gain,
    feedforward_up,
    feedforward_down,
):
    normed = layer_norm(stream, attention_gain[layer_index])
    projected = jnp.dot(
        normed, attention_in[layer_index], preferred_element_type=jnp.float32
    ).astype(jnp.bfloat16)
    mixed_rows = attend(projected, HEADS)
    stream = (
        stream.astype(jnp.float32)
        + jnp.dot(mixed_rows, attention_out[layer_index], preferred_element_type=jnp.float32)
    ).astype(jnp.bfloat16)
    normed = layer_norm(stream, feedforward_gain[layer_index])
    hidden = jax.nn.gelu(
        jnp.dot(normed, feedforward_up[layer_index], preferred_element_type=jnp.float32),
        approximate=False,
    ).astype(jnp.bfloat16)
    return (
        stream.astype(jnp.float32)
        + jnp.dot(hidden, feedforward_down[layer_index], preferred_element_type=jnp.float32)
    ).astype(jnp.bfloat16)


def deliver(row_block, labels, target_device):
    row_count, model_width = row_block.shape
    count_x = lax.axis_size("gx")
    count_y = lax.axis_size("gy")
    peer_count = count_x * count_y
    capacity = 5 * row_count // (2 * peer_count)
    matches = (target_device[:, None] == jnp.arange(peer_count, dtype=jnp.int32)[None, :]).astype(
        jnp.int32
    )
    slot_index = jnp.sum(jnp.cumsum(matches, axis=0) * matches, axis=1) - 1
    target = target_device * capacity + slot_index
    row_buffer = (
        jnp.zeros((peer_count * capacity, model_width), jnp.bfloat16).at[target].set(row_block)
    )
    tag_buffer = jnp.full((peer_count * capacity, 3), -1, jnp.int32).at[target].set(labels)
    received_rows, received_tags = (
        lax.all_to_all(
            row_buffer.reshape(peer_count, capacity, model_width),
            ("gx", "gy"),
            split_axis=0,
            concat_axis=0,
            tiled=True,
        ),
        lax.all_to_all(
            tag_buffer.reshape(peer_count, capacity, 3),
            ("gx", "gy"),
            split_axis=0,
            concat_axis=0,
            tiled=True,
        ),
    )
    received_rows = received_rows.reshape(peer_count * capacity, model_width)
    received_tags = received_tags.reshape(peer_count * capacity, 3)
    landing = jnp.where(received_tags[:, 0] < 0, row_count, received_tags[:, 0])
    placed_rows = (
        jnp.zeros((row_count + 1, model_width), jnp.bfloat16)
        .at[landing]
        .set(received_rows)[:row_count]
    )
    placed_tags = (
        jnp.zeros((row_count + 1, 3), jnp.int32).at[landing].set(received_tags)[:row_count]
    )
    return (placed_rows, placed_tags)


def body(
    features,
    zorder_rank,
    hilbert_rank,
    attention_gain,
    attention_in,
    attention_out,
    feedforward_gain,
    feedforward_up,
    feedforward_down,
):
    weights = (
        attention_gain,
        attention_in,
        attention_out,
        feedforward_gain,
        feedforward_up,
        feedforward_down,
    )
    row_count = features.shape[0]
    my_index = lax.axis_index("gx") * lax.axis_size("gy") + lax.axis_index("gy")
    anchor = my_index * row_count + jnp.arange(row_count, dtype=jnp.int32)
    labels = jnp.stack([zorder_rank % row_count, hilbert_rank, anchor], axis=1)
    current, carried = deliver(features, labels, zorder_rank // row_count)
    current = run_block(current, 0, *weights)
    hilbert_index = carried[:, 1]
    home_index = carried[:, 2]
    labels = jnp.stack([hilbert_index % row_count, home_index, home_index], axis=1)
    current, carried = deliver(current, labels, hilbert_index // row_count)
    home_index = carried[:, 1]
    current = run_block(current, 1, *weights)
    labels = jnp.stack([home_index % row_count, home_index, home_index], axis=1)
    result, leftover = deliver(current, labels, home_index // row_count)
    return result


def solution(mesh):
    in_specs = (
        P(("gx", "gy"), None),
        P(("gx", "gy")),
        P(("gx", "gy")),
        P(),
        P(),
        P(),
        P(),
        P(),
        P(),
    )
    out_specs = P(("gx", "gy"), None)
    return jax.shard_map(body, mesh=mesh, in_specs=in_specs, out_specs=out_specs, check_vma=False)
```

profile of v0, /device:TPU:0, one launch (start us, length us, event | category | flops | bytes accessed | tf_op | source)
XLA Modules:
  0.0 953.9 jit_solution(12620418538200853877)
XLA Ops:
  63.6 33.0 %all-to-all-done.3 = bf16[32,80,512]{2,1,0:T(8,128)(2,1)} async-done(((bf16[32,80,512]{2,1,0:T(8,128)(2,1)}), bf16[32,80,512]{2,1,0:T(8,128)(2,1)}, u32[]{:S(2)}, u32[]{:S(2)}) %all-to-all-start.3) | async-done | bytes 2621472 | tf_op jit(solution)/shard_map/all_to_all | solution.py:92
  124.5 293.4 %while.20 = (s32[]{:T(128)}, bf16[8,1024,4,16]{1,3,2,0:T(8,128)(2,1)S(1)}, bf16[8,3,1024,4,16]{2,4,3,0,1:T(8,128)(2,1)}, s32[]{:T(128)}) while((s32[]{:T(128)}, bf16[8,1024,4,16]{1,3,2,0:T(8,128)(2,1)S(1)}, bf16[8,3,1024,4,16]{2,4,3,0,1:T(8,128)(2,1)}, s32[]{:T(128)}) %tuple.58), condition=%wide.region_21.22_spmd, body=%wide.region_18.21_spmd.sunk | while | flops 306255872 | bytes 68452920 | solution.py:41
  133.7 12.6 %fusion.275 = f32[4,1024]{1,0:T(4,128)S(1)} fusion(f32[4,1024,1024]{1,2,0:T(8,128)} %fusion.274), kind=kOutput, calls=%fused_computation.321.clone.1 | output fusion | flops 16778240 | bytes 16793600 | tf_op jit(solution)/shard_map/while/body/eval_jaxpr/sub | solution.py:35
  146.3 14.9 %fusion.276 = bf16[8,1024,4,16]{1,3,2,0:T(8,128)(2,1)S(1)} fusion(bf16[8,1024,4,16]{1,3,2,0:T(8,128)(2,1)S(1)} %get-tuple-element.143, s32[]{:T(128)} %get-tuple-element.142, f32[4,1024]{1,0:T(4,128)S(1)} %fusion.275, bf16[1,3,1024,4,16]{2,4,3,1,0:T(8,128)(2,1)S(1)} %dynamic-slice_bitcast_fusion.4, f32[4,1024,1024]{1,2,0:T(8,128)} %fusion.274), kind=kOutput, calls=%fused_computation.20.clone.1 | convolution fusion | flops 155259904 | bytes 33833472 | tf_op jit(solution)/shard_map/while/body/eval_jaxpr/hqk,khd->qhd/dot_general | solution.py:37
  170.3 12.6 %fusion.275 = f32[4,1024]{1,0:T(4,128)S(1)} fusion(f32[4,1024,1024]{1,2,0:T(8,128)} %fusion.274), kind=kOutput, calls=%fused_computation.321.clone.1 | output fusion | flops 16778240 | bytes 16793600 | tf_op jit(solution)/shard_map/while/body/eval_jaxpr/sub | solution.py:35
  182.9 14.9 %fusion.276 = bf16[8,1024,4,16]{1,3,2,0:T(8,128)(2,1)S(1)} fusion(bf16[8,1024,4,16]{1,3,2,0:T(8,128)(2,1)S(1)} %get-tuple-element.143, s32[]{:T(128)} %get-tuple-element.142, f32[4,1024]{1,0:T(4,128)S(1)} %fusion.275, bf16[1,3,1024,4,16]{2,4,3,1,0:T(8,128)(2,1)S(1)} %dynamic-slice_bitcast_fusion.4, f32[4,1024,1024]{1,2,0:T(8,128)} %fusion.274), kind=kOutput, calls=%fused_computation.20.clone.1 | convolution fusion | flops 155259904 | bytes 33833472 | tf_op jit(solution)/shard_map/while/body/eval_jaxpr/hqk,khd->qhd/dot_general | solution.py:37
  207.0 12.6 %fusion.275 = f32[4,1024]{1,0:T(4,128)S(1)} fusion(f32[4,1024,1024]{1,2,0:T(8,128)} %fusion.274), kind=kOutput, calls=%fused_computation.321.clone.1 | output fusion | flops 16778240 | bytes 16793600 | tf_op jit(solution)/shard_map/while/body/eval_jaxpr/sub | solution.py:35
  219.6 14.9 %fusion.276 = bf16[8,1024,4,16]{1,3,2,0:T(8,128)(2,1)S(1)} fusion(bf16[8,1024,4,16]{1,3,2,0:T(8,128)(2,1)S(1)} %get-tuple-element.143, s32[]{:T(128)} %get-tuple-element.142, f32[4,1024]{1,0:T(4,128)S(1)} %fusion.275, bf16[1,3,1024,4,16]{2,4,3,1,0:T(8,128)(2,1)S(1)} %dynamic-slice_bitcast_fusion.4, f32[4,1024,1024]{1,2,0:T(8,128)} %fusion.274), kind=kOutput, calls=%fused_computation.20.clone.1 | convolution fusion | flops 155259904 | bytes 33833472 | tf_op jit(solution)/shard_map/while/body/eval_jaxpr/hqk,khd->qhd/dot_general | solution.py:37
  243.6 12.6 %fusion.275 = f32[4,1024]{1,0:T(4,128)S(1)} fusion(f32[4,1024,1024]{1,2,0:T(8,128)} %fusion.274), kind=kOutput, calls=%fused_computation.321.clone.1 | output fusion | flops 16778240 | bytes 16793600 | tf_op jit(solution)/shard_map/while/body/eval_jaxpr/sub | solution.py:35
  256.2 14.9 %fusion.276 = bf16[8,1024,4,16]{1,3,2,0:T(8,128)(2,1)S(1)} fusion(bf16[8,1024,4,16]{1,3,2,0:T(8,128)(2,1)S(1)} %get-tuple-element.143, s32[]{:T(128)} %get-tuple-element.142, f32[4,1024]{1,0:T(4,128)S(1)} %fusion.275, bf16[1,3,1024,4,16]{2,4,3,1,0:T(8,128)(2,1)S(1)} %dynamic-slice_bitcast_fusion.4, f32[4,1024,1024]{1,2,0:T(8,128)} %fusion.274), kind=kOutput, calls=%fused_computation.20.clone.1 | convolution fusion | flops 155259904 | bytes 33833472 | tf_op jit(solution)/shard_map/while/body/eval_jaxpr/hqk,khd->qhd/dot_general | solution.py:37
  280.3 12.6 %fusion.275 = f32[4,1024]{1,0:T(4,128)S(1)} fusion(f32[4,1024,1024]{1,2,0:T(8,128)} %fusion.274), kind=kOutput, calls=%fused_computation.321.clone.1 | output fusion | flops 16778240 | bytes 16793600 | tf_op jit(solution)/shard_map/while/body/eval_jaxpr/sub | solution.py:35
  292.9 14.9 %fusion.276 = bf16[8,1024,4,16]{1,3,2,0:T(8,128)(2,1)S(1)} fusion(bf16[8,1024,4,16]{1,3,2,0:T(8,128)(2,1)S(1)} %get-tuple-element.143, s32[]{:T(128)} %get-tuple-element.142, f32[4,1024]{1,0:T(4,128)S(1)} %fusion.275, bf16[1,3,1024,4,16]{2,4,3,1,0:T(8,128)(2,1)S(1)} %dynamic-slice_bitcast_fusion.4, f32[4,1024,1024]{1,2,0:T(8,128)} %fusion.274), kind=kOutput, calls=%fused_computation.20.clone.1 | convolution fusion | flops 155259904 | bytes 33833472 | tf_op jit(solution)/shard_map/while/body/eval_jaxpr/hqk,khd->qhd/dot_general | solution.py:37
  316.9 12.6 %fusion.275 = f32[4,1024]{1,0:T(4,128)S(1)} fusion(f32[4,1024,1024]{1,2,0:T(8,128)} %fusion.274), kind=kOutput, calls=%fused_computation.321.clone.1 | output fusion | flops 16778240 | bytes 16793600 | tf_op jit(solution)/shard_map/while/body/eval_jaxpr/sub | solution.py:35
  329.5 14.9 %fusion.276 = bf16[8,1024,4,16]{1,3,2,0:T(8,128)(2,1)S(1)} fusion(bf16[8,1024,4,16]{1,3,2,0:T(8,128)(2,1)S(1)} %get-tuple-element.143, s32[]{:T(128)} %get-tuple-element.142, f32[4,1024]{1,0:T(4,128)S(1)} %fusion.275, bf16[1,3,1024,4,16]{2,4,3,1,0:T(8,128)(2,1)S(1)} %dynamic-slice_bitcast_fusion.4, f32[4,1024,1024]{1,2,0:T(8,128)} %fusion.274), kind=kOutput, calls=%fused_computation.20.clone.1 | convolution fusion | flops 155259904 | bytes 33833472 | tf_op jit(solution)/shard_map/while/body/eval_jaxpr/hqk,khd->qhd/dot_general | solution.py:37
  353.6 12.6 %fusion.275 = f32[4,1024]{1,0:T(4,128)S(1)} fusion(f32[4,1024,1024]{1,2,0:T(8,128)} %fusion.274), kind=kOutput, calls=%fused_computation.321.clone.1 | output fusion | flops 16778240 | bytes 16793600 | tf_op jit(solution)/shard_map/while/body/eval_jaxpr/sub | solution.py:35
  366.2 14.9 %fusion.276 = bf16[8,1024,4,16]{1,3,2,0:T(8,128)(2,1)S(1)} fusion(bf16[8,1024,4,16]{1,3,2,0:T(8,128)(2,1)S(1)} %get-tuple-element.143, s32[]{:T(128)} %get-tuple-element.142, f32[4,1024]{1,0:T(4,128)S(1)} %fusion.275, bf16[1,3,1024,4,16]{2,4,3,1,0:T(8,128)(2,1)S(1)} %dynamic-slice_bitcast_fusion.4, f32[4,1024,1024]{1,2,0:T(8,128)} %fusion.274), kind=kOutput, calls=%fused_computation.20.clone.1 | convolution fusion | flops 155259904 | bytes 33833472 | tf_op jit(solution)/shard_map/while/body/eval_jaxpr/hqk,khd->qhd/dot_general | solution.py:37
  390.2 12.6 %fusion.275 = f32[4,1024]{1,0:T(4,128)S(1)} fusion(f32[4,1024,1024]{1,2,0:T(8,128)} %fusion.274), kind=kOutput, calls=%fused_computation.321.clone.1 | output fusion | flops 16778240 | bytes 16793600 | tf_op jit(solution)/shard_map/while/body/eval_jaxpr/sub | solution.py:35
  402.8 14.9 %fusion.276 = bf16[8,1024,4,16]{1,3,2,0:T(8,128)(2,1)S(1)} fusion(bf16[8,1024,4,16]{1,3,2,0:T(8,128)(2,1)S(1)} %get-tuple-element.143, s32[]{:T(128)} %get-tuple-element.142, f32[4,1024]{1,0:T(4,128)S(1)} %fusion.275, bf16[1,3,1024,4,16]{2,4,3,1,0:T(8,128)(2,1)S(1)} %dynamic-slice_bitcast_fusion.4, f32[4,1024,1024]{1,2,0:T(8,128)} %fusion.274), kind=kOutput, calls=%fused_computation.20.clone.1 | convolution fusion | flops 155259904 | bytes 33833472 | tf_op jit(solution)/shard_map/while/body/eval_jaxpr/hqk,khd->qhd/dot_general | solution.py:37
  420.1 23.7 %fusion.85 = bf16[1024,512]{0,1:T(8,128)(2,1)S(1)} fusion(bf16[1024,512]{0,1:T(8,128)(2,1)S(1)} %get-tuple-element.97, bf16[2,2048,512]{2,1,0:T(8,128)(2,1)} %param.21, bf16[2,512,2048]{2,1,0:T(8,128)(2,1)} %param.20, f32[512]{0:T(512)S(1)} %bitcast.217, f32[1024]{0:T(1024)S(1)} %add_rsqrt_fusion.2, f32[1024]{0:T(1024)S(1)} %broadcast_multiply_fusion.2), kind=kOutput, calls=%fused_computation.124 | convolution fusion | flops 4435476480 | bytes 7350272 | tf_op jit(solution)/shard_map/dot_general | solution.py:72
  482.9 34.8 %all-to-all-done.4 = bf16[32,80,512]{2,1,0:T(8,128)(2,1)} async-done(((bf16[32,80,512]{2,1,0:T(8,128)(2,1)}), bf16[32,80,512]{2,1,0:T(8,128)(2,1)}, u32[]{:S(2)}, u32[]{:S(2)}) %all-to-all-start.4) | async-done | bytes 2621472 | tf_op jit(solution)/shard_map/all_to_all | solution.py:92
  545.7 293.5 %while.21 = (s32[]{:T(128)}, bf16[8,1024,4,16]{1,3,2,0:T(8,128)(2,1)S(1)}, bf16[8,3,1024,4,16]{2,4,3,0,1:T(8,128)(2,1)}, s32[]{:T(128)}) while((s32[]{:T(128)}, bf16[8,1024,4,16]{1,3,2,0:T(8,128)(2,1)S(1)}, bf16[8,3,1024,4,16]{2,4,3,0,1:T(8,128)(2,1)}, s32[]{:T(128)}) %tuple.57), condition=%wide.region_31.32_spmd, body=%wide.region_28.31_spmd.sunk | while | flops 306255872 | bytes 68452920 | solution.py:41
  554.9 12.6 %fusion.279 = f32[4,1024]{1,0:T(4,128)S(1)} fusion(f32[4,1024,1024]{1,2,0:T(8,128)} %fusion.278), kind=kOutput, calls=%fused_computation.322.clone.1 | output fusion | flops 16778240 | bytes 16793600 | tf_op jit(solution)/shard_map/while/body/eval_jaxpr/sub | solution.py:35
  567.5 14.9 %fusion.280 = bf16[8,1024,4,16]{1,3,2,0:T(8,128)(2,1)S(1)} fusion(bf16[8,1024,4,16]{1,3,2,0:T(8,128)(2,1)S(1)} %get-tuple-element.155, s32[]{:T(128)} %get-tuple-element.154, f32[4,1024]{1,0:T(4,128)S(1)} %fusion.279, bf16[1,3,1024,4,16]{2,4,3,1,0:T(8,128)(2,1)S(1)} %dynamic-slice_bitcast_fusion.5, f32[4,1024,1024]{1,2,0:T(8,128)} %fusion.278), kind=kOutput, calls=%fused_computation.38.clone.1 | convolution fusion | flops 155259904 | bytes 33833472 | tf_op jit(solution)/shard_map/while/body/eval_jaxpr/hqk,khd->qhd/dot_general | solution.py:37
  604.2 14.9 %fusion.280 = bf16[8,1024,4,16]{1,3,2,0:T(8,128)(2,1)S(1)} fusion(bf16[8,1024,4,16]{1,3,2,0:T(8,128)(2,1)S(1)} %get-tuple-element.155, s32[]{:T(128)} %get-tuple-element.154, f32[4,1024]{1,0:T(4,128)S(1)} %fusion.279, bf16[1,3,1024,4,16]{2,4,3,1,0:T(8,128)(2,1)S(1)} %dynamic-slice_bitcast_fusion.5, f32[4,1024,1024]{1,2,0:T(8,128)} %fusion.278), kind=kOutput, calls=%fused_computation.38.clone.1 | convolution fusion | flops 155259904 | bytes 33833472 | tf_op jit(solution)/shard_map/while/body/eval_jaxpr/hqk,khd->qhd/dot_general | solution.py:37
  640.8 14.9 %fusion.280 = bf16[8,1024,4,16]{1,3,2,0:T(8,128)(2,1)S(1)} fusion(bf16[8,1024,4,16]{1,3,2,0:T(8,128)(2,1)S(1)} %get-tuple-element.155, s32[]{:T(128)} %get-tuple-element.154, f32[4,1024]{1,0:T(4,128)S(1)} %fusion.279, bf16[1,3,1024,4,16]{2,4,3,1,0:T(8,128)(2,1)S(1)} %dynamic-slice_bitcast_fusion.5, f32[4,1024,1024]{1,2,0:T(8,128)} %fusion.278), kind=kOutput, calls=%fused_computation.38.clone.1 | convolution fusion | flops 155259904 | bytes 33833472 | tf_op jit(solution)/shard_map/while/body/eval_jaxpr/hqk,khd->qhd/dot_general | solution.py:37
  677.5 14.9 %fusion.280 = bf16[8,1024,4,16]{1,3,2,0:T(8,128)(2,1)S(1)} fusion(bf16[8,1024,4,16]{1,3,2,0:T(8,128)(2,1)S(1)} %get-tuple-element.155, s32[]{:T(128)} %get-tuple-element.154, f32[4,1024]{1,0:T(4,128)S(1)} %fusion.279, bf16[1,3,1024,4,16]{2,4,3,1,0:T(8,128)(2,1)S(1)} %dynamic-slice_bitcast_fusion.5, f32[4,1024,1024]{1,2,0:T(8,128)} %fusion.278), kind=kOutput, calls=%fused_computation.38.clone.1 | convolution fusion | flops 155259904 | bytes 33833472 | tf_op jit(solution)/shard_map/while/body/eval_jaxpr/hqk,khd->qhd/dot_general | solution.py:37
  714.1 14.9 %fusion.280 = bf16[8,1024,4,16]{1,3,2,0:T(8,128)(2,1)S(1)} fusion(bf16[8,1024,4,16]{1,3,2,0:T(8,128)(2,1)S(1)} %get-tuple-element.155, s32[]{:T(128)} %get-tuple-element.154, f32[4,1024]{1,0:T(4,128)S(1)} %fusion.279, bf16[1,3,1024,4,16]{2,4,3,1,0:T(8,128)(2,1)S(1)} %dynamic-slice_bitcast_fusion.5, f32[4,1024,1024]{1,2,0:T(8,128)} %fusion.278), kind=kOutput, calls=%fused_computation.38.clone.1 | convolution fusion | flops 155259904 | bytes 33833472 | tf_op jit(solution)/shard_map/while/body/eval_jaxpr/hqk,khd->qhd/dot_general | solution.py:37
  750.8 14.9 %fusion.280 = bf16[8,1024,4,16]{1,3,2,0:T(8,128)(2,1)S(1)} fusion(bf16[8,1024,4,16]{1,3,2,0:T(8,128)(2,1)S(1)} %get-tuple-element.155, s32[]{:T(128)} %get-tuple-element.154, f32[4,1024]{1,0:T(4,128)S(1)} %fusion.279, bf16[1,3,1024,4,16]{2,4,3,1,0:T(8,128)(2,1)S(1)} %dynamic-slice_bitcast_fusion.5, f32[4,1024,1024]{1,2,0:T(8,128)} %fusion.278), kind=kOutput, calls=%fused_computation.38.clone.1 | convolution fusion | flops 155259904 | bytes 33833472 | tf_op jit(solution)/shard_map/while/body/eval_jaxpr/hqk,khd->qhd/dot_general | solution.py:37
  787.4 14.9 %fusion.280 = bf16[8,1024,4,16]{1,3,2,0:T(8,128)(2,1)S(1)} fusion(bf16[8,1024,4,16]{1,3,2,0:T(8,128)(2,1)S(1)} %get-tuple-element.155, s32[]{:T(128)} %get-tuple-element.154, f32[4,1024]{1,0:T(4,128)S(1)} %fusion.279, bf16[1,3,1024,4,16]{2,4,3,1,0:T(8,128)(2,1)S(1)} %dynamic-slice_bitcast_fusion.5, f32[4,1024,1024]{1,2,0:T(8,128)} %fusion.278), kind=kOutput, calls=%fused_computation.38.clone.1 | convolution fusion | flops 155259904 | bytes 33833472 | tf_op jit(solution)/shard_map/while/body/eval_jaxpr/hqk,khd->qhd/dot_general | solution.py:37
  824.1 14.9 %fusion.280 = bf16[8,1024,4,16]{1,3,2,0:T(8,128)(2,1)S(1)} fusion(bf16[8,1024,4,16]{1,3,2,0:T(8,128)(2,1)S(1)} %get-tuple-element.155, s32[]{:T(128)} %get-tuple-element.154, f32[4,1024]{1,0:T(4,128)S(1)} %fusion.279, bf16[1,3,1024,4,16]{2,4,3,1,0:T(8,128)(2,1)S(1)} %dynamic-slice_bitcast_fusion.5, f32[4,1024,1024]{1,2,0:T(8,128)} %fusion.278), kind=kOutput, calls=%fused_computation.38.clone.1 | convolution fusion | flops 155259904 | bytes 33833472 | tf_op jit(solution)/shard_map/while/body/eval_jaxpr/hqk,khd->qhd/dot_general | solution.py:37
  841.4 23.8 %fusion.87 = bf16[1024,512]{0,1:T(8,128)(2,1)S(1)} fusion(bf16[1024,512]{0,1:T(8,128)(2,1)S(1)} %get-tuple-element.99, bf16[2,2048,512]{2,1,0:T(8,128)(2,1)} %param.21, bf16[2,512,2048]{2,1,0:T(8,128)(2,1)} %param.20, f32[512]{0:T(512)S(1)} %bitcast.215, f32[1024]{0:T(1024)S(1)} %add_rsqrt_fusion, f32[1024]{0:T(1024)S(1)} %broadcast_multiply_fusion), kind=kOutput, calls=%fused_computation.126 | convolution fusion | flops 4435476480 | bytes 7350272 | tf_op jit(solution)/shard_map/dot_general | solution.py:72
  880.6 58.3 %all-to-all-done.5 = bf16[32,80,512]{2,1,0:T(8,128)(2,1)S(1)} async-done(((bf16[32,80,512]{2,1,0:T(8,128)(2,1)}), bf16[32,80,512]{2,1,0:T(8,128)(2,1)S(1)}, u32[]{:S(2)}, u32[]{:S(2)}) %all-to-all-start.5) | async-done | bytes 2621472 | tf_op jit(solution)/shard_map/all_to_all | solution.py:92
  (179 shorter events, 426.6 us)
Async XLA Ops:
  0.0 36.6 %copy-start.7 = (f32[2,512]{1,0:T(2,128)S(1)}, f32[2,512]{1,0:T(2,128)}, u32[]{:S(2)}) copy-start(f32[2,512]{1,0:T(2,128)} %param.16) | copy-start | bytes 12292
  0.0 37.2 %copy-start.8 = (f32[2,512]{1,0:T(2,128)S(1)}, f32[2,512]{1,0:T(2,128)}, u32[]{:S(2)}) copy-start(f32[2,512]{1,0:T(2,128)} %param.19) | copy-start | bytes 12292
  15.8 14.8 %all-to-all-start = ((s32[32,1,240]{2,1,0:T(1,128)}), s32[32,1,240]{2,1,0:T(1,128)S(1)}, u32[]{:S(2)}, u32[]{:S(2)}) async-start(s32[32,1,240]{2,1,0:T(1,128)} %reshape.341), calls=%async_computation | async-start | bytes 65536 | tf_op jit(solution)/shard_map/all_to_all | solution.py:99
  30.7 66.0 %all-to-all-start.3 = ((bf16[32,80,512]{2,1,0:T(8,128)(2,1)}), bf16[32,80,512]{2,1,0:T(8,128)(2,1)}, u32[]{:S(2)}, u32[]{:S(2)}) async-start(bf16[32,80,512]{2,1,0:T(8,128)(2,1)} %bitcast.24), calls=%async_computation.3 | async-start | bytes 5242880 | tf_op jit(solution)/shard_map/all_to_all | solution.py:92
  58.2 61.5 %copy-start.6 = (s32[1024]{0:T(1024)}, s32[1024]{0:T(1024)S(1)}, u32[]{:S(2)}) copy-start(s32[1024]{0:T(1024)S(1)} %fusion.158) | copy-start | bytes 12292
  96.6 355.2 %all-to-all-start.1 = ((s32[32,1,240]{2,1,0:T(1,128)}), s32[32,1,240]{2,1,0:T(1,128)}, u32[]{:S(2)}, u32[]{:S(2)}) async-start(s32[32,1,240]{2,1,0:T(1,128)} %reshape.343), calls=%async_computation.1 | async-start | bytes 65536 | tf_op jit(solution)/shard_map/all_to_all | solution.py:99
  114.1 5.5 copy-start.2
  124.4 293.5 %copy-start.3 = (bf16[1024,512]{0,1:T(8,128)(2,1)S(1)}, bf16[1024,512]{0,1:T(8,128)(2,1)}, u32[]{:S(2)}) copy-start(bf16[1024,512]{0,1:T(8,128)(2,1)} %copy-done.2) | copy-start | bytes 3145732
  124.5 295.6 %copy-start.11 = (f32[1,512]{1,0:T(1,128)S(1)}, f32[1,512]{1,0:T(1,128)}, u32[]{:S(2)}) copy-start(f32[1,512]{1,0:T(1,128)} %get-tuple-element.91) | copy-start | bytes 6148
  451.8 65.9 %all-to-all-start.4 = ((bf16[32,80,512]{2,1,0:T(8,128)(2,1)}), bf16[32,80,512]{2,1,0:T(8,128)(2,1)}, u32[]{:S(2)}, u32[]{:S(2)}) async-start(bf16[32,80,512]{2,1,0:T(8,128)(2,1)} %bitcast.38), calls=%async_computation.4 | async-start | bytes 5242880 | tf_op jit(solution)/shard_map/all_to_all | solution.py:92
  459.8 76.1 %copy-start.10 = (f32[1,512]{1,0:T(1,128)S(1)}, f32[1,512]{1,0:T(1,128)}, u32[]{:S(2)}) copy-start(f32[1,512]{1,0:T(1,128)} %get-tuple-element.92) | copy-start | bytes 6148
  477.9 63.0 %copy-start.5 = (s32[1024]{0:T(1024)}, s32[1024]{0:T(1024)S(1)}, u32[]{:S(2)}) copy-start(s32[1024]{0:T(1024)S(1)} %get-tuple-element.87) | copy-start | bytes 12292
  517.7 355.3 %all-to-all-start.2 = ((s32[32,1,240]{2,1,0:T(1,128)}), s32[32,1,240]{2,1,0:T(1,128)}, u32[]{:S(2)}, u32[]{:S(2)}) async-start(s32[32,1,240]{2,1,0:T(1,128)} %reshape.345), calls=%async_computation.2 | async-start | bytes 65536 | tf_op jit(solution)/shard_map/all_to_all | solution.py:99
  535.4 5.6 copy-start
  545.7 293.5 %copy-start.1 = (bf16[1024,512]{0,1:T(8,128)(2,1)S(1)}, bf16[1024,512]{0,1:T(8,128)(2,1)}, u32[]{:S(2)}) copy-start(bf16[1024,512]{0,1:T(8,128)(2,1)} %copy-done) | copy-start | bytes 3145732
  545.7 295.7 %copy-start.9 = (f32[1,512]{1,0:T(1,128)S(1)}, f32[1,512]{1,0:T(1,128)}, u32[]{:S(2)}) copy-start(f32[1,512]{1,0:T(1,128)} %get-tuple-element.90) | copy-start | bytes 6148
  873.0 65.8 %all-to-all-start.5 = ((bf16[32,80,512]{2,1,0:T(8,128)(2,1)}), bf16[32,80,512]{2,1,0:T(8,128)(2,1)S(1)}, u32[]{:S(2)}, u32[]{:S(2)}) async-start(bf16[32,80,512]{2,1,0:T(8,128)(2,1)} %bitcast.52), calls=%async_computation.5 | async-start | bytes 5242880 | tf_op jit(solution)/shard_map/all_to_all | solution.py:92
  938.8 1.5 copy-start.4
where the time goes:
time: 964 us; the launch traced here: 954 us
  matrix products  430 us (45%)
  other arithmetic  247 us (26%)
  waiting for transfers between devices  126 us (13%)
  local copies, waits for them, and re-layouts  116 us (12%)
  starting transfers between devices  34 us (4%)
    dot_general x16, matrix products, one_group(): jnp.einsum('hqk,khd->qhd', weights, part[2], preferred_element_type=jnp.f...  239 us
    sub x16, other arithmetic, one_group(): raised = jnp.exp(scores - row_max)  201 us
    dot_general x16, matrix products, one_group(): jnp.einsum('qhd,khd->hqk', part[0], part[1], preferred_element_type=jnp.f...  129 us
    all_to_all x3, waiting for transfers between devices, deliver(): lax.all_to_all(row_buffer.reshape(peer_count, capacity, model_width), ('g...  126 us
    dot_general x2, matrix products, run_block(): jnp.dot(hidden, feedforward_down[layer_index], preferred_element_type=jnp...  47.5 us
    scatter x3, local copies, waits for them, and re-layouts, deliver(): placed_rows = jnp.zeros((row_count + 1, model_width), jnp.bfloat16).at[la...  36.9 us
    another operation x9, other arithmetic  27.4 us
    scatter x3, local copies, waits for them, and re-layouts, deliver(): jnp.zeros((peer_count * capacity, model_width), jnp.bfloat16).at[target]  22.3 us
  transfers between devices with their start and end apart: 6, of which 3 were waited for; matrix products, arithmetic and copies ran while one was open for 80% of the time, Pallas kernels for 0%

commit v1 on v0

v1 whole, which is shorter than its diff:
```python
import functools

import jax
import jax.numpy as jnp
from jax import lax
from jax.experimental import pallas as pl
from jax.experimental.pallas import tpu as pltpu
from jax.sharding import PartitionSpec as P

HEADS = 32
PATCH = 1024
EPSILON = 1e-05
LOG2E = 1.4426950408889634
AXES = ("gx", "gy")
SAFE_EXPONENT = 80.0

bf16 = jnp.bfloat16
f32 = jnp.float32
i32 = jnp.int32


def call(kernel, name, out_shape, scratch=(), flops=0):
    def run(*args):
        vmem = pl.BlockSpec(memory_space=pltpu.VMEM)
        outs = jax.tree.map(lambda _: vmem, out_shape)
        moved = sum(a.size * a.dtype.itemsize for a in args)
        return pl.pallas_call(
            kernel,
            name=name,
            out_shape=out_shape,
            in_specs=[vmem] * len(args),
            out_specs=outs,
            scratch_shapes=scratch,
            compiler_params=pltpu.CompilerParams(vmem_limit_bytes=56 << 20),
            cost_estimate=pl.CostEstimate(flops=flops, bytes_accessed=moved, transcendentals=0),
        )(*args)

    return run


def column(row):
    return jnp.broadcast_to(row, (128, row.shape[1])).T


def order_in_bucket(keys, size):
    shift = size.bit_length() - 1
    tall = column(keys)
    pieces = []
    for start in range(0, keys.shape[1], 128):
        piece = keys[:, start : start + 128]
        low = lax.shift_left(lax.shift_right_logical(piece, shift), shift)
        inside = jnp.logical_and(tall >= low, tall < piece)
        pieces.append(jnp.sum(jnp.where(inside, 1.0, 0.0), axis=0, keepdims=True))
    return jnp.concatenate(pieces, axis=1).astype(i32)


def digits(*values):
    rows = []
    for value, count in values:
        for place in range(count):
            rows.append(
                jnp.bitwise_and(lax.shift_right_logical(value, 8 * place), 255).astype(f32)
            )
    rows += [jnp.zeros_like(rows[0])] * (8 - len(rows))
    return jnp.concatenate(rows, axis=0).astype(bf16)


def undigits(rows, start, count):
    value = rows[start : start + 1].astype(i32)
    for place in range(1, count):
        value = value + lax.shift_left(rows[start + place : start + place + 1].astype(i32), 8 * place)
    return value


def chosen(wanted, axis, start, rows, columns):
    index = lax.broadcasted_iota(i32, (rows, columns), axis) + start
    return jnp.where(wanted == index, 1.0, 0.0).astype(bf16)


def contract_last(a, b):
    return lax.dot_general(a, b, (((1,), (1,)), ((), ())), preferred_element_type=f32)


def send_tags_kernel(size, capacity, zr_ref, hr_ref, z_tag_ref, h_tag_ref, target_ref, home_ref):
    shift = size.bit_length() - 1
    zr, hr = zr_ref[...], hr_ref[...]
    row = lax.broadcasted_iota(i32, (1, size), 1)
    z_owner = lax.shift_right_logical(zr, shift)
    h_owner = lax.shift_right_logical(hr, shift)
    target = z_owner * capacity + order_in_bucket(z_owner * size + row, size)
    home = h_owner * capacity + order_in_bucket(hr, size)
    target_ref[...] = target
    home_ref[...] = home
    ones = jnp.ones_like(zr)
    for wanted, near, far, tag_ref in ((target, zr, hr, z_tag_ref), (home, hr, zr, h_tag_ref)):
        parts = digits((jnp.bitwise_and(near, size - 1), 2), (far, 3), (ones, 1))
        slots = tag_ref.shape[1]
        for start in range(0, slots, 512):
            picked = contract_last(parts, chosen(wanted, 0, start, 512, size))
            near_value = undigits(picked, 0, 2)
            far_value = undigits(picked, 2, 3)
            there = picked[5:6] > 0.5
            tag_ref[:, start : start + 512] = jnp.where(there, far_value * size + near_value, -1)


def route_kernel(size, capacity, z_tag_ref, h_tag_ref, place_ref, target2_ref, source2_ref, target3_ref):
    shift = size.bit_length() - 1
    slots = z_tag_ref.shape[1]
    z_tag, h_tag = z_tag_ref[...], h_tag_ref[...]
    z_place = jnp.where(z_tag < 0, -1, jnp.bitwise_and(z_tag, size - 1))
    h_place = jnp.where(h_tag < 0, -1, jnp.bitwise_and(h_tag, size - 1))
    place_ref[...] = z_place
    slot = lax.broadcasted_iota(i32, (1, slots), 1)
    peer = jnp.zeros((1, slots), f32)
    peer = jnp.floor((slot.astype(f32) + 0.5) * (1.0 / capacity)).astype(i32)
    z_parts = digits((lax.shift_right_logical(jnp.maximum(z_tag, 0), shift), 3))
    h_parts = digits((lax.shift_right_logical(jnp.maximum(h_tag, 0), shift), 3), (peer, 1))
    z_pieces, h_pieces = [], []
    for start in range(0, size, 256):
        z_pieces.append(contract_last(z_parts, chosen(z_place, 0, start, 256, slots)))
        h_pieces.append(contract_last(h_parts, chosen(h_place, 0, start, 256, slots)))
    z_rows = jnp.concatenate(z_pieces, axis=1)
    h_rows = jnp.concatenate(h_pieces, axis=1)
    row = lax.broadcasted_iota(i32, (1, size), 1)
    owner = lax.shift_right_logical(undigits(z_rows, 0, 3), shift)
    target2_ref[...] = owner * capacity + order_in_bucket(owner * size + row, size)
    zr = undigits(h_rows, 0, 3)
    source2_ref[...] = lax.shift_right_logical(zr, shift) * capacity + order_in_bucket(zr, size)
    home = undigits(h_rows, 3, 1)
    target3_ref[...] = home * capacity + order_in_bucket(home * size + row, size)


def pack_rows(target, rows, out_ref):
    slots = out_ref.shape[0]

    def step(i, carry):
        start = pl.multiple_of(i * 256, 256)
        pick = chosen(target, 0, start, 256, rows.shape[0])
        out_ref[pl.ds(start, 256), :] = jnp.dot(
            pick, rows, preferred_element_type=f32
        ).astype(bf16)
        return carry

    lax.fori_loop(0, slots // 256, step, 0, unroll=2)


def pack_kernel(target_ref, rows_ref, out_ref):
    pack_rows(target_ref[...], rows_ref[...], out_ref)


def unpack_kernel(source_ref, received_ref, out_ref, tall_ref):
    slots = received_ref.shape[0]
    tall_ref[...] = column(source_ref[...])

    def step(i, carry):
        start = pl.multiple_of(i * 256, 256)
        tall = tall_ref[pl.ds(start, 256), :]
        pick = jnp.concatenate(
            [chosen(tall, 1, piece, 256, 128) for piece in range(0, slots, 128)], axis=1
        )
        out_ref[pl.ds(start, 256), :] = jnp.dot(
            pick, received_ref[...], preferred_element_type=f32
        ).astype(bf16)
        return carry

    lax.fori_loop(0, out_ref.shape[0] // 256, step, 0, unroll=2)


def normalize(values, gain):
    values = values.astype(f32)
    centred = values - jnp.mean(values, axis=-1, keepdims=True)
    variance = jnp.mean(centred * centred, axis=-1, keepdims=True)
    return (centred * lax.rsqrt(variance + EPSILON) * gain).astype(bf16)


def project_kernel(
    by_source, heads, index_ref, received_ref, gain_ref, weight_ref,
    rows_ref, q_ref, k_ref, vt_ref, bound_ref, tall_ref,
):
    slots, width = received_ref.shape
    head_size = width // heads
    scale = head_size ** (-0.5) * LOG2E
    if by_source:
        tall_ref[...] = column(index_ref[...])
    group = jnp.where(
        lax.broadcasted_iota(i32, (width, 128), 0) // head_size
        == lax.broadcasted_iota(i32, (width, 128), 1),
        1.0,
        0.0,
    ).astype(bf16)
    block = 256

    def step(i, carry):
        q_most, k_most = carry
        start = pl.multiple_of(i * block, block)
        if by_source:
            tall = tall_ref[pl.ds(start, block), :]
            pick = jnp.concatenate(
                [chosen(tall, 1, piece, block, 128) for piece in range(0, slots, 128)], axis=1
            )
        else:
            pick = chosen(index_ref[...], 0, start, block, slots)
        rows = jnp.dot(pick, received_ref[...], preferred_element_type=f32).astype(bf16)
        rows_ref[pl.ds(start, block), :] = rows
        normed = normalize(rows, gain_ref[...])
        q = (
            jnp.dot(normed, weight_ref[:, :width], preferred_element_type=f32) * scale
        ).astype(bf16)
        k = jnp.dot(normed, weight_ref[:, width : 2 * width], preferred_element_type=f32).astype(bf16)
        v = jnp.dot(normed, weight_ref[:, 2 * width :], preferred_element_type=f32)
        q_ref[pl.ds(start, block), :] = q
        k_ref[pl.ds(start, block), :] = k
        vt_ref[:, pl.ds(start, block)] = v.T.astype(bf16)
        q_size = jnp.dot(q * q, group, preferred_element_type=f32)
        k_size = jnp.dot(k * k, group, preferred_element_type=f32)
        q_most = jnp.maximum(q_most, jnp.max(q_size, axis=0, keepdims=True))
        k_most = jnp.maximum(k_most, jnp.max(k_size, axis=0, keepdims=True))
        return q_most, k_most

    zero = jnp.zeros((1, 128), f32)
    q_most, k_most = lax.fori_loop(0, rows_ref.shape[0] // block, step, (zero, zero))
    bound_ref[...] = q_most * k_most


def attend_kernel(heads, q_ref, k_ref, vt_ref, bound_ref, out_ref):
    size, width = q_ref.shape
    head_size = width // heads
    per_group = 128 // head_size
    lane_head = lax.broadcasted_iota(i32, (1, 128), 1) // head_size
    none = jnp.zeros((), bf16)
    ones = jnp.ones((16, size), bf16)

    def operands(head):
        group = pl.multiple_of((head // per_group) * 128, 128)
        mine = lane_head == head % per_group
        keys = jnp.where(mine, k_ref[:, pl.ds(group, 128)], none)
        first = pl.multiple_of(head * head_size, head_size)
        values = jnp.concatenate([vt_ref[pl.ds(first, head_size), :], ones], axis=0)
        return group, first, keys, values

    def finish(first, start, count, values, weights):
        mixed = jnp.dot(values, weights, preferred_element_type=f32)
        out_ref[pl.ds(first, head_size), pl.ds(start, count)] = (
            mixed[:head_size] / mixed[head_size : head_size + 1]
        ).astype(bf16)

    together = 2

    def small_scores(i, carry):
        for part in range(together):
            group, first, keys, values = operands(i * together + part)
            scores = contract_last(keys, q_ref[:, pl.ds(group, 128)])
            finish(first, 0, size, values, jnp.exp2(scores).astype(bf16))
        return carry

    def any_scores(head, carry):
        group, first, keys, values = operands(head)

        def tile(t, inner):
            start = pl.multiple_of(t * 256, 256)
            scores = contract_last(keys, q_ref[pl.ds(start, 256), pl.ds(group, 128)])
            scores = scores - jnp.max(scores, axis=0, keepdims=True)
            finish(first, start, 256, values, jnp.exp2(scores).astype(bf16))
            return inner

        return lax.fori_loop(0, size // 256, tile, carry)

    small = jnp.max(bound_ref[...]) <= SAFE_EXPONENT * SAFE_EXPONENT

    @pl.when(small)
    def _():
        lax.fori_loop(0, heads // together, small_scores, 0)

    @pl.when(jnp.logical_not(small))
    def _():
        lax.fori_loop(0, heads, any_scores, 0)


def gelu(x):
    size = jnp.abs(x)
    t = 1.0 / (1.0 + (0.3275911 * 0.7071067811865476) * size)
    series = 0.5 * 1.061405429
    for coefficient in (-1.453152027, 1.421413741, -0.284496736, 0.254829592):
        series = series * t + 0.5 * coefficient
    tail = series * t * jnp.exp2((x * x) * (-0.5 * LOG2E))
    return jnp.maximum(x, 0.0) - size * tail


def feed_kernel(
    target_ref, rows_ref, mixed_ref, out_weight_ref, gain_ref, up_ref, down_ref, packed_ref, block_ref
):
    size, width = rows_ref.shape
    hidden = up_ref.shape[1]
    block = 256
    piece = 512

    def step(i, carry):
        start = pl.multiple_of(i * block, block)
        mixed = lax.dot_general(
            mixed_ref[:, pl.ds(start, block)],
            out_weight_ref[...],
            (((0,), (0,)), ((), ())),
            preferred_element_type=f32,
        )
        stream = (rows_ref[pl.ds(start, block), :].astype(f32) + mixed).astype(bf16)
        normed = normalize(stream, gain_ref[...])
        total = stream.astype(f32)
        for first in range(0, hidden, piece):
            up = jnp.dot(normed, up_ref[:, first : first + piece], preferred_element_type=f32)
            total = total + jnp.dot(
                gelu(up).astype(bf16), down_ref[first : first + piece, :], preferred_element_type=f32
            )
        block_ref[pl.ds(start, block), :] = total.astype(bf16)
        return carry

    lax.fori_loop(0, size // block, step, 0)
    pack_rows(target_ref[...], block_ref[...], packed_ref)


def exchange(packed, peers):
    slots, width = packed.shape
    received = lax.all_to_all(
        packed.reshape(peers, slots // peers, width), AXES, split_axis=0, concat_axis=0, tiled=True
    )
    return received.reshape(slots, width)


def body(
    features, zorder_rank, hilbert_rank, attention_gain, attention_in, attention_out,
    feedforward_gain, feedforward_up, feedforward_down,
):
    size, width = features.shape
    peers = lax.axis_size("gx") * lax.axis_size("gy")
    capacity = 5 * size // (2 * peers)
    slots = peers * capacity
    hidden = feedforward_up.shape[2]

    def shape(rows, columns, dtype):
        return jax.ShapeDtypeStruct((rows, columns), dtype)

    index = shape(1, size, i32)
    tags = shape(1, slots, i32)
    z_tags, h_tags, target1, source3 = call(
        functools.partial(send_tags_kernel, size, capacity), "send_tags", (tags, tags, index, index)
    )(zorder_rank.reshape(1, size), hilbert_rank.reshape(1, size))
    both = jnp.concatenate([z_tags.reshape(peers, 1, capacity), h_tags.reshape(peers, 1, capacity)], axis=2)
    both = lax.all_to_all(both, AXES, split_axis=0, concat_axis=0, tiled=True)
    z_tags = both[:, 0, :capacity].reshape(1, slots)
    h_tags = both[:, 0, capacity:].reshape(1, slots)
    select = 2 * slots * size * width
    packed = call(pack_kernel, "pack", shape(slots, width, bf16), flops=select)(target1, features)
    received = exchange(packed, peers)
    place1, target2, source2, target3 = call(
        functools.partial(route_kernel, size, capacity), "route", (tags, index, index, index)
    )(z_tags, h_tags)

    for layer, incoming, outgoing in ((0, place1, target2), (1, source2, target3)):
        half = shape(size, width, bf16)
        rows, q, k, vt, bound = call(
            functools.partial(project_kernel, layer == 1, HEADS),
            "project",
            (half, half, half, shape(width, size, bf16), shape(1, 128, f32)),
            scratch=[pltpu.VMEM((size, 128), i32)],
            flops=select + 6 * size * width * width,
        )(incoming, received, attention_gain[layer].reshape(1, width), attention_in[layer])
        mixed = call(
            functools.partial(attend_kernel, HEADS),
            "attend",
            shape(width, size, bf16),
            flops=16 * size * size * width,
        )(q, k, vt, bound)
        packed = call(
            feed_kernel,
            "feed",
            shape(slots, width, bf16),
            scratch=[pltpu.VMEM((size, width), bf16)],
            flops=select + 2 * size * width * (width + 2 * hidden),
        )(
            outgoing, rows, mixed, attention_out[layer], feedforward_gain[layer].reshape(1, width),
            feedforward_up[layer], feedforward_down[layer],
        )
        received = exchange(packed, peers)

    return call(
        unpack_kernel,
        "unpack",
        shape(size, width, bf16),
        scratch=[pltpu.VMEM((size, 128), i32)],
        flops=select,
    )(source3, received)


def solution(mesh):
    split = P(AXES, None)
    return jax.shard_map(
        body,
        mesh=mesh,
        in_specs=(split, P(AXES), P(AXES), P(), P(), P(), P(), P(), P()),
        out_specs=split,
        check_vma=False,
    )
```

time: 964 us -> 477 us (0.49); the launches traced: 954 us -> 477 us
  matrix products: 430 us -> 0 us
  Pallas kernels: 0 us -> 278 us
  other arithmetic: 247 us -> 2.22 us
  blocking collectives: 0 us -> 129 us
  local copies, waits for them, and re-layouts: 116 us -> 14.5 us
  waiting for transfers between devices: 126 us -> 40.5 us
  starting transfers between devices: 34 us -> 12.4 us
    dot_general x38 -> x0, matrix products: 430 us -> none  [the longest x16 239 us: one_group(): jnp.einsum('hqk,khd->qhd', weights, part[2], preferred_element_type=jnp.f...]
    pallas_call x0 -> x10, Pallas kernels: none -> 278 us  [run(): pl.pallas_call(kernel, name=name, out_shape=out_shape, in_specs=[vmem] *...]
    sub x18 -> x0, other arithmetic: 201 us -> none  [the longest x16 201 us: one_group(): raised = jnp.exp(scores - row_max)]
    all_to_all x0 -> x2, blocking collectives: none -> 129 us  [exchange(): lax.all_to_all(packed.reshape(peers, slots // peers, width), AXES, split_...]
    all_to_all x6 -> x2, waiting for transfers between devices: 126 us -> 40.5 us  [the longest x1 39.7 us: exchange(): lax.all_to_all(packed.reshape(peers, slots // peers, width), AXES, split_...]
    scatter x9 -> x0, local copies, waits for them, and re-layouts: 76.5 us -> none  [the longest x3 36.9 us: deliver(): placed_rows = jnp.zeros((row_count + 1, model_width), jnp.bfloat16).at[la...]
    another operation x10 -> x0, other arithmetic: 28.1 us -> none
    all_to_all x6 -> x2, starting transfers between devices: 34 us -> 12.4 us  [the longest x1 7.33 us: body(): both = lax.all_to_all(both, AXES, split_axis=0, concat_axis=0, tiled=True)]
  transfers between devices with their start and end apart: 6 -> 2, of which waited for: 3 -> 2; matrix products, arithmetic and copies ran while one was open for 80% -> 2% of each run, Pallas kernels for 0% -> 3%
where the time goes in v1:
time: 477 us
  Pallas kernels  278 us (58%)
  blocking collectives  129 us (27%)
  waiting for transfers between devices  40.5 us (8%)
  local copies, waits for them, and re-layouts  14.5 us (3%)
  starting transfers between devices  12.4 us (3%)
    pallas_call x10, Pallas kernels, run(): pl.pallas_call(kernel, name=name, out_shape=out_shape, in_specs=[vmem] *...  278 us
    all_to_all x2, blocking collectives, exchange(): lax.all_to_all(packed.reshape(peers, slots // peers, width), AXES, split_...  129 us
    all_to_all x1, waiting for transfers between devices, exchange(): lax.all_to_all(packed.reshape(peers, slots // peers, width), AXES, split_...  39.7 us
  transfers between devices with their start and end apart: 2, of which 2 were waited for; matrix products, arithmetic and copies ran while one was open for 2% of the time, Pallas kernels for 3%

profile of v1, /device:TPU:0, one launch (start us, length us, event | category | flops | bytes accessed | tf_op | source)
XLA Modules:
  0.0 476.8 jit_solution(14270352633399185211)
XLA Ops:
  0.0 5.4 %send_tags.1 = (s32[1,2560]{1,0:T(1,128)}, s32[1,2560]{1,0:T(1,128)}, s32[1,1024]{1,0:T(1,128)}, s32[1,1024]{1,0:T(1,128)}) custom-call(s32[1,1024]{1,0:T(1,128)} %bitcast.33, s32[1,1024]{1,0:T(1,128)} %bitcast.34), custom_call_target="tpu_custom_call" | custom-call | bytes 8192 | tf_op jit(solution)/shard_map/send_tags/pallas_call | solution.py:27
  5.4 0.7 reduce
  6.2 0.7 reduce.1
  6.9 0.1 reshape.33
  7.0 0.1 reshape.32
  7.0 0.8 pad_add_fusion
  7.8 7.3 %all-to-all-start = ((s32[32,1,160]{2,1,0:T(1,128)}), s32[32,1,160]{2,1,0:T(1,128)S(1)}, u32[]{:S(2)}, u32[]{:S(2)}) async-start(s32[32,1,160]{2,1,0:T(1,128)} %pad_add_fusion), calls=%async_computation | async-start | bytes 65536 | tf_op jit(solution)/shard_map/all_to_all | solution.py:347
  15.1 6.4 %pack.1 = bf16[2560,512]{1,0:T(8,128)(2,1)} custom-call(s32[1,1024]{1,0:T(1,128)} %get-tuple-element.30.target_ref, bf16[1024,512]{1,0:T(8,128)(2,1)} %rows_ref.1), custom_call_target="tpu_custom_call" | custom-call | flops 2684354560 | bytes 1052672 | tf_op jit(solution)/shard_map/pack/pallas_call | solution.py:27
  21.5 0.8 all-to-all-done
  22.4 5.1 %all-to-all-start.1 = ((bf16[32,80,512]{2,1,0:T(8,128)(2,1)}), bf16[32,80,512]{2,1,0:T(8,128)(2,1)}, u32[]{:S(2)}, u32[]{:S(2)}) async-start(bf16[32,80,512]{2,1,0:T(8,128)(2,1)} %bitcast.26), calls=%async_computation.1 | async-start | bytes 5242880 | tf_op jit(solution)/shard_map/all_to_all | solution.py:322
  27.5 0.6 fusion.1
  28.1 0.6 fusion
  28.8 2.3 slice_bitcast_fusion.6
  31.0 1.8 slice_bitcast_fusion.4
  32.9 1.5 copy-done
  34.4 2.7 slice_bitcast_fusion.1
  37.0 1.0 copy-done.1
  38.1 2.3 slice_bitcast_fusion
  40.4 0.1 slice_reduce_fusion
  40.5 0.7 reshape_squeeze.7.h_tag_ref
  41.2 0.7 reshape_squeeze.6.z_tag_ref
  41.9 6.0 %route.1 = (s32[1,2560]{1,0:T(1,128)}, s32[1,1024]{1,0:T(1,128)}, s32[1,1024]{1,0:T(1,128)}, s32[1,1024]{1,0:T(1,128)}) custom-call(s32[1,2560]{1,0:T(1,128)} %reshape_squeeze.6.z_tag_ref, s32[1,2560]{1,0:T(1,128)} %reshape_squeeze.7.h_tag_ref), custom_call_target="tpu_custom_call" | custom-call | bytes 20480 | tf_op jit(solution)/shard_map/route/pallas_call | solution.py:27
  47.9 39.7 %all-to-all-done.1 = bf16[32,80,512]{2,1,0:T(8,128)(2,1)} async-done(((bf16[32,80,512]{2,1,0:T(8,128)(2,1)}), bf16[32,80,512]{2,1,0:T(8,128)(2,1)}, u32[]{:S(2)}, u32[]{:S(2)}) %all-to-all-start.1) | async-done | bytes 2621472 | tf_op jit(solution)/shard_map/all_to_all | solution.py:322
  87.6 10.3 %project.2 = (bf16[1024,512]{1,0:T(8,128)(2,1)}, bf16[1024,512]{1,0:T(8,128)(2,1)}, bf16[1024,512]{1,0:T(8,128)(2,1)}, bf16[512,1024]{1,0:T(8,128)(2,1)}, f32[1,128]{1,0:T(1,128)}) custom-call(s32[1,2560]{1,0:T(1,128)} %get-tuple-element.29.index_ref, bf16[2560,512]{1,0:T(8,128)(2,1)} %bitcast.5.received_ref, f32[1,512]{1,0:T(1,128)} %get-tuple-element.54.gain_ref, ...), custom_call_target="tpu_custom_call" | custom-call | flops 4294967296 | bytes 4206592 | tf_op jit(solution)/shard_map/project/pallas_call | solution.py:27
  97.8 96.0 %attend.2.mixed_ref = bf16[512,1024]{1,0:T(8,128)(2,1)} custom-call(bf16[1024,512]{1,0:T(8,128)(2,1)} %get-tuple-element.32.q_ref, bf16[1024,512]{1,0:T(8,128)(2,1)} %get-tuple-element.33.k_ref, bf16[512,1024]{1,0:T(8,128)(2,1)} %get-tuple-element.34.vt_ref, f32[1,128]{1,0:T(1,128)} %get-tuple-element.35.bound_ref), custom_call_target="tpu_custom_call" | custom-call | flops 8589934592 | bytes 3146240 | tf_op jit(solution)/shard_map/attend/pallas_call | solution.py:27
  193.8 20.8 %feed.2 = bf16[2560,512]{1,0:T(8,128)(2,1)} custom-call(s32[1,1024]{1,0:T(1,128)} %get-tuple-element.28.target_ref, bf16[1024,512]{1,0:T(8,128)(2,1)} %get-tuple-element.31.rows_ref, bf16[512,1024]{1,0:T(8,128)(2,1)} %attend.2.mixed_ref, bf16[512,512]{1,0:T(8,128)(2,1)} %get-tuple-element.50.out_weight_ref, f32[1,512]{1,0:T(1,128)} %get-tuple-element.52.gain_ref, ...), custom_call_target="tpu_custom_call" | custom-call | flops 7516192768 | bytes 6821888 | tf_op jit(solution)/shard_map/feed/pallas_call | solution.py:27
  214.6 65.1 %all_to_all.20 = bf16[32,80,512]{2,1,0:T(8,128)(2,1)} all-to-all(bf16[32,80,512]{2,1,0:T(8,128)(2,1)} %bitcast.28), channel_id=1, replica_groups=mesh['gx'=8,'gy'=4] {'gx','gy'}, dimensions={0} | all-to-all | bytes 5242880 | tf_op jit(solution)/shard_map/all_to_all | solution.py:322
  279.7 10.4 %project.3 = (bf16[1024,512]{1,0:T(8,128)(2,1)}, bf16[1024,512]{1,0:T(8,128)(2,1)}, bf16[1024,512]{1,0:T(8,128)(2,1)}, bf16[512,1024]{1,0:T(8,128)(2,1)}, f32[1,128]{1,0:T(1,128)}) custom-call(s32[1,1024]{1,0:T(1,128)} %get-tuple-element.27.index_ref, bf16[2560,512]{1,0:T(8,128)(2,1)} %bitcast.27, f32[1,512]{1,0:T(1,128)} %get-tuple-element.53.gain_ref, ...), custom_call_target="tpu_custom_call" | custom-call | flops 4294967296 | bytes 4200448 | tf_op jit(solution)/shard_map/project/pallas_call | solution.py:27
  290.1 95.8 %attend.3.mixed_ref = bf16[512,1024]{1,0:T(8,128)(2,1)} custom-call(bf16[1024,512]{1,0:T(8,128)(2,1)} %get-tuple-element.37.q_ref, bf16[1024,512]{1,0:T(8,128)(2,1)} %get-tuple-element.38.k_ref, bf16[512,1024]{1,0:T(8,128)(2,1)} %get-tuple-element.39.vt_ref, f32[1,128]{1,0:T(1,128)} %get-tuple-element.40.bound_ref), custom_call_target="tpu_custom_call" | custom-call | flops 8589934592 | bytes 3146240 | tf_op jit(solution)/shard_map/attend/pallas_call | solution.py:27
  385.9 20.8 %feed.3 = bf16[2560,512]{1,0:T(8,128)(2,1)} custom-call(s32[1,1024]{1,0:T(1,128)} %get-tuple-element.26.target_ref, bf16[1024,512]{1,0:T(8,128)(2,1)} %get-tuple-element.36.rows_ref, bf16[512,1024]{1,0:T(8,128)(2,1)} %attend.3.mixed_ref, bf16[512,512]{1,0:T(8,128)(2,1)} %get-tuple-element.49.out_weight_ref, f32[1,512]{1,0:T(1,128)} %get-tuple-element.51.gain_ref, ...), custom_call_target="tpu_custom_call" | custom-call | flops 7516192768 | bytes 6821888 | tf_op jit(solution)/shard_map/feed/pallas_call | solution.py:27
  406.8 64.1 %all_to_all.21 = bf16[32,80,512]{2,1,0:T(8,128)(2,1)} all-to-all(bf16[32,80,512]{2,1,0:T(8,128)(2,1)} %bitcast.29), channel_id=1, replica_groups=mesh['gx'=8,'gy'=4] {'gx','gy'}, dimensions={0} | all-to-all | bytes 5242880 | tf_op jit(solution)/shard_map/all_to_all | solution.py:322
  470.8 6.0 %unpack.1 = bf16[1024,512]{1,0:T(8,128)(2,1)} custom-call(s32[1,1024]{1,0:T(1,128)} %get-tuple-element.23.source_ref, bf16[2560,512]{1,0:T(8,128)(2,1)} %bitcast.30), custom_call_target="tpu_custom_call" | custom-call | flops 2684354560 | bytes 2625536 | tf_op jit(solution)/shard_map/unpack/pallas_call | solution.py:27
  (8 shorter events, 0.0 us)
Async XLA Ops:
  7.8 14.6 %all-to-all-start = ((s32[32,1,160]{2,1,0:T(1,128)}), s32[32,1,160]{2,1,0:T(1,128)S(1)}, u32[]{:S(2)}, u32[]{:S(2)}) async-start(s32[32,1,160]{2,1,0:T(1,128)} %pad_add_fusion), calls=%async_computation | async-start | bytes 65536 | tf_op jit(solution)/shard_map/all_to_all | solution.py:347
  22.4 5.1 %copy-start.3 = (f32[2,512]{1,0:T(2,128)S(1)}, f32[2,512]{1,0:T(2,128)}, u32[]{:S(2)}) copy-start(f32[2,512]{1,0:T(2,128)} %param.12) | copy-start | bytes 12292
  22.4 5.8 %copy-start.4 = (f32[2,512]{1,0:T(2,128)S(1)}, f32[2,512]{1,0:T(2,128)}, u32[]{:S(2)}) copy-start(f32[2,512]{1,0:T(2,128)} %param.15) | copy-start | bytes 12292
  22.4 8.7 %copy-start.2 = (bf16[2,512,1536]{2,1,0:T(8,128)(2,1)S(1)}, bf16[2,512,1536]{2,1,0:T(8,128)(2,1)}, u32[]{:S(2)}) copy-start(bf16[2,512,1536]{2,1,0:T(8,128)(2,1)} %param.13) | copy-start | bytes 9437188
  22.4 65.2 %all-to-all-start.1 = ((bf16[32,80,512]{2,1,0:T(8,128)(2,1)}), bf16[32,80,512]{2,1,0:T(8,128)(2,1)}, u32[]{:S(2)}, u32[]{:S(2)}) async-start(bf16[32,80,512]{2,1,0:T(8,128)(2,1)} %bitcast.26), calls=%async_computation.1 | async-start | bytes 5242880 | tf_op jit(solution)/shard_map/all_to_all | solution.py:322
  31.0 3.3 copy-start
  34.4 3.7 copy-start.1

commit v2 on v1

--- a/solution.py
+++ b/solution.py
@@ -91,16 +91,29 @@
     home = h_owner * capacity + order_in_bucket(hr, size)
     target_ref[...] = target
     home_ref[...] = home
+    peers = z_tag_ref.shape[0]
     ones = jnp.ones_like(zr)
-    for wanted, near, far, tag_ref in ((target, zr, hr, z_tag_ref), (home, hr, zr, h_tag_ref)):
-        parts = digits((jnp.bitwise_and(near, size - 1), 2), (far, 3), (ones, 1))
-        slots = tag_ref.shape[1]
-        for start in range(0, slots, 512):
-            picked = contract_last(parts, chosen(wanted, 0, start, 512, size))
-            near_value = undigits(picked, 0, 2)
-            far_value = undigits(picked, 2, 3)
-            there = picked[5:6] > 0.5
-            tag_ref[:, start : start + 512] = jnp.where(there, far_value * size + near_value, -1)
+    peer = lax.broadcasted_iota(i32, (peers, 1), 0)
+    lane = lax.broadcasted_iota(i32, (128, 1), 0)
+    for owner, wanted, near, far, tag_ref in (
+        (z_owner, target, zr, hr, z_tag_ref),
+        (h_owner, home, hr, zr, h_tag_ref),
+    ):
+        place = wanted - owner * capacity
+        parts = digits((jnp.bitwise_and(near, size - 1), 2), (far, 3), (ones, 1)).astype(f32)
+        mine = jnp.where(owner == peer, 1.0, 0.0)
+        spread = jnp.where(place == lane, 1.0, 0.0).astype(bf16)
+        tall = jnp.concatenate([mine * parts[d : d + 1] for d in range(6)], axis=0).astype(bf16)
+        found = contract_last(tall, spread).astype(i32)
+
+        def value(first, count):
+            total = found[first * peers : (first + 1) * peers]
+            for d in range(1, count):
+                low = (first + d) * peers
+                total = total + lax.shift_left(found[low : low + peers], 8 * d)
+            return total
+
+        tag_ref[...] = jnp.where(value(5, 1) > 0, value(2, 3) * size + value(0, 2), -1)
 
 
 def route_kernel(size, capacity, z_tag_ref, h_tag_ref, place_ref, target2_ref, source2_ref, target3_ref):
@@ -173,13 +186,89 @@
     return (centred * lax.rsqrt(variance + EPSILON) * gain).astype(bf16)
 
 
-def project_kernel(
-    by_source, heads, index_ref, received_ref, gain_ref, weight_ref,
-    rows_ref, q_ref, k_ref, vt_ref, bound_ref, tall_ref,
+def attend(heads, small, q_ref, k_ref, vt_ref, out_ref):
+    size, width = q_ref.shape
+    head_size = width // heads
+    per_group = 128 // head_size
+    lane_head = lax.broadcasted_iota(i32, (1, 128), 1) // head_size
+    none = jnp.zeros((), bf16)
+    ones = jnp.ones((16, size), bf16)
+
+    def operands(head):
+        group = pl.multiple_of((head // per_group) * 128, 128)
+        mine = lane_head == head % per_group
+        keys = jnp.where(mine, k_ref[:, pl.ds(group, 128)], none)
+        first = pl.multiple_of(head * head_size, head_size)
+        values = jnp.concatenate([vt_ref[pl.ds(first, head_size), :], ones], axis=0)
+        return group, first, keys, values
+
+    def finish(first, start, count, values, weights):
+        mixed = jnp.dot(values, weights, preferred_element_type=f32)
+        out_ref[pl.ds(first, head_size), pl.ds(start, count)] = (
+            mixed[:head_size] / mixed[head_size : head_size + 1]
+        ).astype(bf16)
+
+    together = 2
+
+    def small_scores(i, carry):
+        for part in range(together):
+            group, first, keys, values = operands(i * together + part)
+            scores = contract_last(keys, q_ref[:, pl.ds(group, 128)])
+            finish(first, 0, size, values, jnp.exp2(scores).astype(bf16))
+        return carry
+
+    def any_scores(head, carry):
+        group, first, keys, values = operands(head)
+
+        def tile(t, inner):
+            start = pl.multiple_of(t * 256, 256)
+            scores = contract_last(keys, q_ref[pl.ds(start, 256), pl.ds(group, 128)])
+            scores = scores - jnp.max(scores, axis=0, keepdims=True)
+            finish(first, start, 256, values, jnp.exp2(scores).astype(bf16))
+            return inner
+
+        return lax.fori_loop(0, size // 256, tile, carry)
+
+    @pl.when(small)
+    def _():
+        lax.fori_loop(0, heads // together, small_scores, 0)
+
+    @pl.when(jnp.logical_not(small))
+    def _():
+        lax.fori_loop(0, heads, any_scores, 0)
+
+
+def gelu(x):
+    return (0.5 * x) * (1.0 + lax.erf(x * 0.7071067811865476))
+
+
+def block_kernel(
+    layer, by_source, heads,
+    index_ref, target_ref, gain_in_ref, gain_feed_ref,
+    received_hbm, in_hbm, out_hbm, up_hbm, down_hbm,
+    packed_hbm,
+    received_ref, in_ref, out_ref, up_ref, down_ref, packed_ref,
+    rows_ref, q_ref, k_ref, vt_ref, mixed_ref, block_ref, tall_ref, load_sem, store_sem,
 ):
     slots, width = received_ref.shape
+    size = rows_ref.shape[0]
+    hidden = up_ref.shape[1]
     head_size = width // heads
     scale = head_size ** (-0.5) * LOG2E
+    loads = [
+        pltpu.make_async_copy(source, target, load_sem.at[i])
+        for i, (source, target) in enumerate(
+            (
+                (received_hbm, received_ref),
+                (in_hbm.at[layer], in_ref),
+                (out_hbm.at[layer], out_ref),
+                (up_hbm.at[layer], up_ref),
+                (down_hbm.at[layer], down_ref),
+            )
+        )
+    ]
+    for load in loads:
+        load.start()
     if by_source:
         tall_ref[...] = column(index_ref[...])
     group = jnp.where(
@@ -189,8 +278,10 @@
         0.0,
     ).astype(bf16)
     block = 256
-
-    def step(i, carry):
+    loads[0].wait()
+    loads[1].wait()
+
+    def project(i, carry):
         q_most, k_most = carry
         start = pl.multiple_of(i * block, block)
         if by_source:
@@ -202,12 +293,12 @@
             pick = chosen(index_ref[...], 0, start, block, slots)
         rows = jnp.dot(pick, received_ref[...], preferred_element_type=f32).astype(bf16)
         rows_ref[pl.ds(start, block), :] = rows
-        normed = normalize(rows, gain_ref[...])
+        normed = normalize(rows, gain_in_ref[...])
         q = (
-            jnp.dot(normed, weight_ref[:, :width], preferred_element_type=f32) * scale
+            jnp.dot(normed, in_ref[:, :width], preferred_element_type=f32) * scale
         ).astype(bf16)
-        k = jnp.dot(normed, weight_ref[:, width : 2 * width], preferred_element_type=f32).astype(bf16)
-        v = jnp.dot(normed, weight_ref[:, 2 * width :], preferred_element_type=f32)
+        k = jnp.dot(normed, in_ref[:, width : 2 * width], preferred_element_type=f32).astype(bf16)
+        v = jnp.dot(normed, in_ref[:, 2 * width :], preferred_element_type=f32)
         q_ref[pl.ds(start, block), :] = q
         k_ref[pl.ds(start, block), :] = k
         vt_ref[:, pl.ds(start, block)] = v.T.astype(bf16)
@@ -218,92 +309,23 @@
         return q_most, k_most
 
     zero = jnp.zeros((1, 128), f32)
-    q_most, k_most = lax.fori_loop(0, rows_ref.shape[0] // block, step, (zero, zero))
-    bound_ref[...] = q_most * k_most
-
-
-def attend_kernel(heads, q_ref, k_ref, vt_ref, bound_ref, out_ref):
-    size, width = q_ref.shape
-    head_size = width // heads
-    per_group = 128 // head_size
-    lane_head = lax.broadcasted_iota(i32, (1, 128), 1) // head_size
-    none = jnp.zeros((), bf16)
-    ones = jnp.ones((16, size), bf16)
-
-    def operands(head):
-        group = pl.multiple_of((head // per_group) * 128, 128)
-        mine = lane_head == head % per_group
-        keys = jnp.where(mine, k_ref[:, pl.ds(group, 128)], none)
-        first = pl.multiple_of(head * head_size, head_size)
-        values = jnp.concatenate([vt_ref[pl.ds(first, head_size), :], ones], axis=0)
-        return group, first, keys, values
-
-    def finish(first, start, count, values, weights):
-        mixed = jnp.dot(values, weights, preferred_element_type=f32)
-        out_ref[pl.ds(first, head_size), pl.ds(start, count)] = (
-            mixed[:head_size] / mixed[head_size : head_size + 1]
-        ).astype(bf16)
-
-    together = 2
-
-    def small_scores(i, carry):
-        for part in range(together):
-            group, first, keys, values = operands(i * together + part)
-            scores = contract_last(keys, q_ref[:, pl.ds(group, 128)])
-            finish(first, 0, size, values, jnp.exp2(scores).astype(bf16))
-        return carry
-
-    def any_scores(head, carry):
-        group, first, keys, values = operands(head)
-
-        def tile(t, inner):
-            start = pl.multiple_of(t * 256, 256)
-            scores = contract_last(keys, q_ref[pl.ds(start, 256), pl.ds(group, 128)])
-            scores = scores - jnp.max(scores, axis=0, keepdims=True)
-            finish(first, start, 256, values, jnp.exp2(scores).astype(bf16))
-            return inner
-
-        return lax.fori_loop(0, size // 256, tile, carry)
-
-    small = jnp.max(bound_ref[...]) <= SAFE_EXPONENT * SAFE_EXPONENT
-
-    @pl.when(small)
-    def _():
-        lax.fori_loop(0, heads // together, small_scores, 0)
-
-    @pl.when(jnp.logical_not(small))
-    def _():
-        lax.fori_loop(0, heads, any_scores, 0)
-
-
-def gelu(x):
-    size = jnp.abs(x)
-    t = 1.0 / (1.0 + (0.3275911 * 0.7071067811865476) * size)
-    series = 0.5 * 1.061405429
-    for coefficient in (-1.453152027, 1.421413741, -0.284496736, 0.254829592):
-        series = series * t + 0.5 * coefficient
-    tail = series * t * jnp.exp2((x * x) * (-0.5 * LOG2E))
-    return jnp.maximum(x, 0.0) - size * tail
-
-
-def feed_kernel(
-    target_ref, rows_ref, mixed_ref, out_weight_ref, gain_ref, up_ref, down_ref, packed_ref, block_ref
-):
-    size, width = rows_ref.shape
-    hidden = up_ref.shape[1]
-    block = 256
+    q_most, k_most = lax.fori_loop(0, size // block, project, (zero, zero), unroll=2)
+    small = jnp.max(q_most * k_most) <= SAFE_EXPONENT * SAFE_EXPONENT
+    attend(heads, small, q_ref, k_ref, vt_ref, mixed_ref)
+    for load in loads[2:]:
+        load.wait()
     piece = 512
 
-    def step(i, carry):
+    def feed(i, carry):
         start = pl.multiple_of(i * block, block)
         mixed = lax.dot_general(
             mixed_ref[:, pl.ds(start, block)],
-            out_weight_ref[...],
+            out_ref[...],
             (((0,), (0,)), ((), ())),
             preferred_element_type=f32,
         )
         stream = (rows_ref[pl.ds(start, block), :].astype(f32) + mixed).astype(bf16)
-        normed = normalize(stream, gain_ref[...])
+        normed = normalize(stream, gain_feed_ref[...])
         total = stream.astype(f32)
         for first in range(0, hidden, piece):
             up = jnp.dot(normed, up_ref[:, first : first + piece], preferred_element_type=f32)
@@ -313,8 +335,62 @@
         block_ref[pl.ds(start, block), :] = total.astype(bf16)
         return carry
 
-    lax.fori_loop(0, size // block, step, 0)
-    pack_rows(target_ref[...], block_ref[...], packed_ref)
+    lax.fori_loop(0, size // block, feed, 0, unroll=2)
+    stores = []
+    for i, start in enumerate(range(0, slots, 256)):
+        pick = chosen(target_ref[...], 0, start, 256, size)
+        packed_ref[start : start + 256, :] = jnp.dot(
+            pick, block_ref[...], preferred_element_type=f32
+        ).astype(bf16)
+        stores.append(
+            pltpu.make_async_copy(
+                packed_ref.at[pl.ds(start, 256)], packed_hbm.at[pl.ds(start, 256)], store_sem.at[i]
+            )
+        )
+        stores[-1].start()
+    for store in stores:
+        store.wait()
+
+
+def run_block(layer, by_source, index, target, received, gains_in, w_in, w_out, gains_feed, up, down):
+    slots, width = received.shape
+    size = target.shape[1]
+    hidden = up.shape[2]
+    vmem = pl.BlockSpec(memory_space=pltpu.VMEM)
+    hbm = pl.BlockSpec(memory_space=pl.ANY)
+    half = pltpu.VMEM((size, width), bf16)
+    flops = 4 * slots * size * width + size * width * (8 * width + 4 * hidden + 16 * size)
+    return pl.pallas_call(
+        functools.partial(block_kernel, layer, by_source, HEADS),
+        name="block",
+        out_shape=jax.ShapeDtypeStruct((slots, width), bf16),
+        in_specs=[vmem] * 4 + [hbm] * 5,
+        out_specs=hbm,
+        scratch_shapes=[
+            pltpu.VMEM((slots, width), bf16),
+            pltpu.VMEM((width, 3 * width), bf16),
+            pltpu.VMEM((width, width), bf16),
+            pltpu.VMEM((width, hidden), bf16),
+            pltpu.VMEM((hidden, width), bf16),
+            pltpu.VMEM((slots, width), bf16),
+            half,
+            half,
+            half,
+            pltpu.VMEM((width, size), bf16),
+            pltpu.VMEM((width, size), bf16),
+            half,
+            pltpu.VMEM((size, 128), i32),
+            pltpu.SemaphoreType.DMA((5,)),
+            pltpu.SemaphoreType.DMA((slots // 256,)),
+        ],
+        compiler_params=pltpu.CompilerParams(vmem_limit_bytes=56 << 20),
+        cost_estimate=pl.CostEstimate(
+            flops=flops, bytes_accessed=4 * slots * width, transcendentals=0
+        ),
+    )(
+        index, target, gains_in[layer].reshape(1, width), gains_feed[layer].reshape(1, width),
+        received, w_in, w_out, up, down,
+    )
 
 
 def exchange(packed, peers):
@@ -333,20 +409,20 @@
     peers = lax.axis_size("gx") * lax.axis_size("gy")
     capacity = 5 * size // (2 * peers)
     slots = peers * capacity
-    hidden = feedforward_up.shape[2]
 
     def shape(rows, columns, dtype):
         return jax.ShapeDtypeStruct((rows, columns), dtype)
 
     index = shape(1, size, i32)
     tags = shape(1, slots, i32)
+    sent = shape(peers, 128, i32)
     z_tags, h_tags, target1, source3 = call(
-        functools.partial(send_tags_kernel, size, capacity), "send_tags", (tags, tags, index, index)
+        functools.partial(send_tags_kernel, size, capacity), "send_tags", (sent, sent, index, index)
     )(zorder_rank.reshape(1, size), hilbert_rank.reshape(1, size))
-    both = jnp.concatenate([z_tags.reshape(peers, 1, capacity), h_tags.reshape(peers, 1, capacity)], axis=2)
+    both = jnp.concatenate([z_tags, h_tags], axis=1).reshape(peers, 1, 256)
     both = lax.all_to_all(both, AXES, split_axis=0, concat_axis=0, tiled=True)
     z_tags = both[:, 0, :capacity].reshape(1, slots)
-    h_tags = both[:, 0, capacity:].reshape(1, slots)
+    h_tags = both[:, 0, 128 : 128 + capacity].reshape(1, slots)
     select = 2 * slots * size * width
     packed = call(pack_kernel, "pack", shape(slots, width, bf16), flops=select)(target1, features)
     received = exchange(packed, peers)
@@ -355,29 +431,9 @@
     )(z_tags, h_tags)
 
     for layer, incoming, outgoing in ((0, place1, target2), (1, source2, target3)):
-        half = shape(size, width, bf16)
-        rows, q, k, vt, bound = call(
-            functools.partial(project_kernel, layer == 1, HEADS),
-            "project",
-            (half, half, half, shape(width, size, bf16), shape(1, 128, f32)),
-            scratch=[pltpu.VMEM((size, 128), i32)],
-            flops=select + 6 * size * width * width,
-        )(incoming, received, attention_gain[layer].reshape(1, width), attention_in[layer])
-        mixed = call(
-            functools.partial(attend_kernel, HEADS),
-            "attend",
-            shape(width, size, bf16),
-            flops=16 * size * size * width,
-        )(q, k, vt, bound)
-        packed = call(
-            feed_kernel,
-            "feed",
-            shape(slots, width, bf16),
-            scratch=[pltpu.VMEM((size, width), bf16)],
-            flops=select + 2 * size * width * (width + 2 * hidden),
-        )(
-            outgoing, rows, mixed, attention_out[layer], feedforward_gain[layer].reshape(1, width),
-            feedforward_up[layer], feedforward_down[layer],
+        packed = run_block(
+            layer, layer == 1, incoming, outgoing, received, attention_gain, attention_in,
+            attention_out, feedforward_gain, feedforward_up, feedforward_down,
         )
         received = exchange(packed, peers)
 

time: 477 us -> 451 us (0.945)
  Pallas kernels: 278 us -> 251 us
  waiting for transfers between devices: 40.5 us -> 52.8 us
  local copies, waits for them, and re-layouts: 14.5 us -> 4.21 us
    pallas_call x10 -> x4, Pallas kernels: 278 us -> 21.5 us  [run(): pl.pallas_call(kernel, name=name, out_shape=out_shape, in_specs=[vmem] *...]
    pallas_call x0 -> x2, Pallas kernels: none -> 229 us  [run_block(): pl.pallas_call(functools.partial(block_kernel, layer, by_source, HEADS),...]
    all_to_all x1, waiting for transfers between devices: 39.7 us -> 52 us  [exchange(): lax.all_to_all(packed.reshape(peers, slots // peers, width), AXES, split_...]
    squeeze x4 -> x0, local copies, waits for them, and re-layouts: 9.1 us -> none  [the longest x1 2.66 us: body(): feedforward_up[layer]]
  transfers between devices with their start and end apart: 2 -> 2, of which waited for: 2 -> 2; matrix products, arithmetic and copies ran while one was open for 2% -> 0% of each run, Pallas kernels for 3% -> 3%
where the time goes in v2:
time: 451 us; the launch traced here: 450 us
  Pallas kernels  251 us (56%)
  blocking collectives  129 us (29%)
  waiting for transfers between devices  52.8 us (12%)
  starting transfers between devices  12.3 us (3%)
    pallas_call x2, Pallas kernels, run_block(): pl.pallas_call(functools.partial(block_kernel, layer, by_source, HEADS),...  229 us
    all_to_all x2, blocking collectives, exchange(): lax.all_to_all(packed.reshape(peers, slots // peers, width), AXES, split_...  129 us
    all_to_all x1, waiting for transfers between devices, exchange(): lax.all_to_all(packed.reshape(peers, slots // peers, width), AXES, split_...  52 us
    pallas_call x4, Pallas kernels, run(): pl.pallas_call(kernel, name=name, out_shape=out_shape, in_specs=[vmem] *...  21.5 us
  transfers between devices with their start and end apart: 2, of which 2 were waited for; matrix products, arithmetic and copies ran while one was open for 0% of the time, Pallas kernels for 3%

profile of v2, /device:TPU:0, one launch (start us, length us, event | category | flops | bytes accessed | tf_op | source)
XLA Modules:
  0.0 450.1 jit_solution(609925520908301494)
XLA Ops:
  0.0 3.1 send_tags.1
  3.1 0.7 add_bitcast_fusion
  3.9 0.6 copy.10
  4.5 7.3 %all-to-all-start = ((s32[32,1,256]{2,1,0:T(1,128)}), s32[32,1,256]{2,1,0:T(1,128)S(1)}, u32[]{:S(2)}, u32[]{:S(2)}) async-start(s32[32,1,256]{2,1,0:T(1,128)} %copy.10), calls=%async_computation | async-start | bytes 65536 | tf_op jit(solution)/shard_map/all_to_all | solution.py:423
  11.9 6.4 %pack.1 = bf16[2560,512]{1,0:T(8,128)(2,1)} custom-call(s32[1,1024]{1,0:T(1,128)} %get-tuple-element.20.target_ref, bf16[1024,512]{1,0:T(8,128)(2,1)} %rows_ref.1), custom_call_target="tpu_custom_call" | custom-call | flops 2684354560 | bytes 1052672 | tf_op jit(solution)/shard_map/pack/pallas_call | solution.py:27
  18.3 0.8 all-to-all-done
  19.1 0.0 copy-start.1
  19.1 0.0 copy-start.2
  19.1 5.0 %all-to-all-start.1 = ((bf16[32,80,512]{2,1,0:T(8,128)(2,1)}), bf16[32,80,512]{2,1,0:T(8,128)(2,1)S(1)}, u32[]{:S(2)}, u32[]{:S(2)}) async-start(bf16[32,80,512]{2,1,0:T(8,128)(2,1)} %bitcast.10), calls=%async_computation.1 | async-start | bytes 5242880 | tf_op jit(solution)/shard_map/all_to_all | solution.py:398
  24.1 0.0 copy-done.1
  24.2 0.0 copy-done.2
  24.2 0.6 fusion
  24.8 0.1 slice_reduce_fusion
  24.9 0.7 reshape_squeeze.6.z_tag_ref
  25.5 0.7 reshape_squeeze.7.h_tag_ref
  26.2 6.0 %route.1 = (s32[1,2560]{1,0:T(1,128)}, s32[1,1024]{1,0:T(1,128)}, s32[1,1024]{1,0:T(1,128)}, s32[1,1024]{1,0:T(1,128)}) custom-call(s32[1,2560]{1,0:T(1,128)} %reshape_squeeze.6.z_tag_ref, s32[1,2560]{1,0:T(1,128)} %reshape_squeeze.7.h_tag_ref), custom_call_target="tpu_custom_call" | custom-call | bytes 20480 | tf_op jit(solution)/shard_map/route/pallas_call | solution.py:27
  32.2 52.0 %all-to-all-done.1 = bf16[32,80,512]{2,1,0:T(8,128)(2,1)S(1)} async-done(((bf16[32,80,512]{2,1,0:T(8,128)(2,1)}), bf16[32,80,512]{2,1,0:T(8,128)(2,1)S(1)}, u32[]{:S(2)}, u32[]{:S(2)}) %all-to-all-start.1) | async-done | bytes 2621472 | tf_op jit(solution)/shard_map/all_to_all | solution.py:398
  84.2 0.0 copy-start
  84.2 1.5 copy-done
  85.7 114.7 %block.2 = bf16[2560,512]{1,0:T(8,128)(2,1)} custom-call(s32[1,2560]{1,0:T(1,128)} %get-tuple-element.18.index_ref, s32[1,1024]{1,0:T(1,128)} %get-tuple-element.19.target_ref, f32[1,512]{1,0:T(1,128)} %get-tuple-element.28.gain_in_ref, f32[1,512]{1,0:T(1,128)} %get-tuple-element.23.gain_feed_ref, bf16[2560,512]{1,0:T(8,128)(2,1)} %bitcast.11, ...), custom_call_target="tpu_custom_call" | custom-call | flops 20401094656 | bytes 5242880 | tf_op jit(solution)/shard_map/block/pallas_call | solution.py:363
  200.4 65.1 %all_to_all.20 = bf16[32,80,512]{2,1,0:T(8,128)(2,1)} all-to-all(bf16[32,80,512]{2,1,0:T(8,128)(2,1)} %bitcast.13), channel_id=1, replica_groups=mesh['gx'=8,'gy'=4] {'gx','gy'}, dimensions={0} | all-to-all | bytes 5242880 | tf_op jit(solution)/shard_map/all_to_all | solution.py:398
  265.5 114.6 %block.3 = bf16[2560,512]{1,0:T(8,128)(2,1)} custom-call(s32[1,1024]{1,0:T(1,128)} %get-tuple-element.16.index_ref, s32[1,1024]{1,0:T(1,128)} %get-tuple-element.17.target_ref, f32[1,512]{1,0:T(1,128)} %get-tuple-element.27.gain_in_ref, f32[1,512]{1,0:T(1,128)} %get-tuple-element.24.gain_feed_ref, bf16[2560,512]{1,0:T(8,128)(2,1)} %bitcast.12, ...), custom_call_target="tpu_custom_call" | custom-call | flops 20401094656 | bytes 5242880 | tf_op jit(solution)/shard_map/block/pallas_call | solution.py:363
  380.1 64.1 %all_to_all.21 = bf16[32,80,512]{2,1,0:T(8,128)(2,1)} all-to-all(bf16[32,80,512]{2,1,0:T(8,128)(2,1)} %bitcast.14), channel_id=1, replica_groups=mesh['gx'=8,'gy'=4] {'gx','gy'}, dimensions={0} | all-to-all | bytes 5242880 | tf_op jit(solution)/shard_map/all_to_all | solution.py:398
  444.2 6.0 %unpack.1 = bf16[1024,512]{1,0:T(8,128)(2,1)} custom-call(s32[1,1024]{1,0:T(1,128)} %get-tuple-element.13.source_ref, bf16[2560,512]{1,0:T(8,128)(2,1)} %bitcast.15), custom_call_target="tpu_custom_call" | custom-call | flops 2684354560 | bytes 2625536 | tf_op jit(solution)/shard_map/unpack/pallas_call | solution.py:27
Async XLA Ops:
  4.5 14.6 %all-to-all-start = ((s32[32,1,256]{2,1,0:T(1,128)}), s32[32,1,256]{2,1,0:T(1,128)S(1)}, u32[]{:S(2)}, u32[]{:S(2)}) async-start(s32[32,1,256]{2,1,0:T(1,128)} %copy.10), calls=%async_computation | async-start | bytes 65536 | tf_op jit(solution)/shard_map/all_to_all | solution.py:423
  19.1 5.0 %copy-start.1 = (f32[2,512]{1,0:T(2,128)S(1)}, f32[2,512]{1,0:T(2,128)}, u32[]{:S(2)}) copy-start(f32[2,512]{1,0:T(2,128)} %param.15) | copy-start | bytes 12292
  19.1 5.0 %copy-start.2 = (f32[2,512]{1,0:T(2,128)S(1)}, f32[2,512]{1,0:T(2,128)}, u32[]{:S(2)}) copy-start(f32[2,512]{1,0:T(2,128)} %param.12) | copy-start | bytes 12292
  19.1 65.0 %all-to-all-start.1 = ((bf16[32,80,512]{2,1,0:T(8,128)(2,1)}), bf16[32,80,512]{2,1,0:T(8,128)(2,1)S(1)}, u32[]{:S(2)}, u32[]{:S(2)}) async-start(bf16[32,80,512]{2,1,0:T(8,128)(2,1)} %bitcast.10), calls=%async_computation.1 | async-start | bytes 5242880 | tf_op jit(solution)/shard_map/all_to_all | solution.py:398
  84.2 1.5 copy-start

commit v3 on v2

--- a/solution.py
+++ b/solution.py
@@ -81,25 +81,37 @@
     return lax.dot_general(a, b, (((1,), (1,)), ((), ())), preferred_element_type=f32)
 
 
-def send_tags_kernel(size, capacity, zr_ref, hr_ref, z_tag_ref, h_tag_ref, target_ref, home_ref):
+def my_index():
+    return lax.axis_index("gx") * lax.axis_size("gy") + lax.axis_index("gy")
+
+
+def turned(index, peers):
+    half = peers // 2
+    return jnp.where(index >= half, 2 * (index - half) + 1, 2 * index)
+
+
+def turned_back(index, peers):
+    return index // 2 + (index % 2) * (peers // 2)
+
+
+def send_tags_kernel(size, capacity, zr_ref, hr_ref, tag_ref, target_ref, source_ref):
     shift = size.bit_length() - 1
+    peers = tag_ref.shape[0]
     zr, hr = zr_ref[...], hr_ref[...]
     row = lax.broadcasted_iota(i32, (1, size), 1)
     z_owner = lax.shift_right_logical(zr, shift)
     h_owner = lax.shift_right_logical(hr, shift)
-    target = z_owner * capacity + order_in_bucket(z_owner * size + row, size)
-    home = h_owner * capacity + order_in_bucket(hr, size)
-    target_ref[...] = target
-    home_ref[...] = home
-    peers = z_tag_ref.shape[0]
+    z_place = order_in_bucket(z_owner * size + row, size)
+    h_place = order_in_bucket(hr, size)
+    me = turned(my_index(), peers)
+    target_ref[...] = jnp.bitwise_xor(turned(z_owner, peers), me) * capacity + z_place
+    source_ref[...] = jnp.bitwise_xor(turned(h_owner, peers), me) * capacity + h_place
     ones = jnp.ones_like(zr)
     peer = lax.broadcasted_iota(i32, (peers, 1), 0)
     lane = lax.broadcasted_iota(i32, (128, 1), 0)
-    for owner, wanted, near, far, tag_ref in (
-        (z_owner, target, zr, hr, z_tag_ref),
-        (h_owner, home, hr, zr, h_tag_ref),
+    for i, (owner, place, near, far) in enumerate(
+        ((z_owner, z_place, zr, hr), (h_owner, h_place, hr, zr))
     ):
-        place = wanted - owner * capacity
         parts = digits((jnp.bitwise_and(near, size - 1), 2), (far, 3), (ones, 1)).astype(f32)
         mine = jnp.where(owner == peer, 1.0, 0.0)
         spread = jnp.where(place == lane, 1.0, 0.0).astype(bf16)
@@ -113,57 +125,160 @@
                 total = total + lax.shift_left(found[low : low + peers], 8 * d)
             return total
 
-        tag_ref[...] = jnp.where(value(5, 1) > 0, value(2, 3) * size + value(0, 2), -1)
-
-
-def route_kernel(size, capacity, z_tag_ref, h_tag_ref, place_ref, target2_ref, source2_ref, target3_ref):
+        tag_ref[:, i * 128 : (i + 1) * 128] = jnp.where(
+            value(5, 1) > 0, value(2, 3) * size + value(0, 2), -1
+        )
+
+
+def from_xor(table, me):
+    peers = table.shape[0]
+    row = lax.broadcasted_iota(i32, table.shape, 0)
+    bit = 1
+    while bit < peers:
+        up = pltpu.roll(table, peers - bit, 0)
+        down = pltpu.roll(table, bit, 0)
+        swapped = jnp.where(jnp.bitwise_and(row, bit) == 0, up, down)
+        table = jnp.where(jnp.bitwise_and(me, bit) == 0, table, swapped)
+        bit *= 2
+    return table
+
+
+def offsets(counts):
+    peers = counts.shape[0]
+    row = lax.broadcasted_iota(i32, counts.shape, 0)
+    total = counts
+    step = 1
+    while step < peers:
+        total = total + jnp.where(row >= step, pltpu.roll(total, step, 0), 0)
+        step *= 2
+    return total - counts
+
+
+def positions_of_slots(counts, first, capacity, slots):
+    peers = counts.shape[0]
+    owner = lax.broadcasted_iota(i32, (peers, 128), 0)
+    pieces = []
+    for start in range(0, slots, 128):
+        slot = lax.broadcasted_iota(i32, (peers, 128), 1) + start
+        place = slot - owner * capacity
+        mine = jnp.logical_and(place >= 0, place < counts)
+        pieces.append(jnp.sum(jnp.where(mine, first + place + 1, 0), axis=0, keepdims=True) - 1)
+    return jnp.concatenate(pieces, axis=1)
+
+
+def listed(tags, size):
+    peers = tags.shape[0]
+    counts = jnp.sum(jnp.where(tags >= 0, 1.0, 0.0), axis=1, keepdims=True).astype(i32)
+    counts = jnp.broadcast_to(counts, (peers, 128))
+    first = offsets(counts)
+    position = lax.broadcasted_iota(i32, (1, size), 1)
+    wide_first = jnp.concatenate([first] * (size // 128), axis=1)
+    wide_end = jnp.concatenate([first + counts] * (size // 128), axis=1)
+    within = jnp.logical_and(position >= wide_first, position < wide_end)
+    mine = jnp.where(within, 1.0, 0.0)
+    owner_index = lax.broadcasted_iota(i32, (peers, size), 0)
+    owner = jnp.sum(jnp.where(within, owner_index, 0), axis=0, keepdims=True)
+    place = position - jnp.sum(jnp.where(within, wide_first, 0), axis=0, keepdims=True)
+    at_place = lax.broadcasted_iota(i32, (128, size), 0) == place
     shift = size.bit_length() - 1
-    slots = z_tag_ref.shape[1]
-    z_tag, h_tag = z_tag_ref[...], h_tag_ref[...]
-    z_place = jnp.where(z_tag < 0, -1, jnp.bitwise_and(z_tag, size - 1))
-    h_place = jnp.where(h_tag < 0, -1, jnp.bitwise_and(h_tag, size - 1))
-    place_ref[...] = z_place
-    slot = lax.broadcasted_iota(i32, (1, slots), 1)
-    peer = jnp.zeros((1, slots), f32)
-    peer = jnp.floor((slot.astype(f32) + 0.5) * (1.0 / capacity)).astype(i32)
-    z_parts = digits((lax.shift_right_logical(jnp.maximum(z_tag, 0), shift), 3))
-    h_parts = digits((lax.shift_right_logical(jnp.maximum(h_tag, 0), shift), 3), (peer, 1))
-    z_pieces, h_pieces = [], []
+    clean = jnp.maximum(tags, 0)
+    near, far = jnp.bitwise_and(clean, size - 1), lax.shift_right_logical(clean, shift)
+    mine = mine.astype(bf16)
+
+    def fetch(values, count):
+        total = jnp.zeros((1, size), i32)
+        for d in range(count):
+            digit = jnp.bitwise_and(lax.shift_right_logical(values, 8 * d), 255)
+            spread = lax.dot_general(
+                digit.astype(f32).astype(bf16), mine, (((0,), (0,)), ((), ())),
+                preferred_element_type=f32,
+            )
+            picked = jnp.sum(jnp.where(at_place, spread, 0.0), axis=0, keepdims=True)
+            total = total + lax.shift_left(picked.astype(i32), 8 * d)
+        return total
+
+    return owner, fetch(near, 2), fetch(far, 3), counts, first
+
+
+def route_kernel(
+    size, capacity, tag_ref, place1_ref, target2_ref, place2_ref, target3_ref
+):
+    shift = size.bit_length() - 1
+    slots = place1_ref.shape[1]
+    peers = tag_ref.shape[0]
+    me = turned(my_index(), peers)
+    tags = from_xor(tag_ref[...], me)
+    owner, zs, hr, counts, first = listed(tags[:, :128], size)
+    place1_ref[...] = positions_of_slots(counts, first, capacity, slots)
+    goal = jnp.bitwise_xor(turned(lax.shift_right_logical(hr, shift), peers), me)
+    target2_ref[...] = goal * capacity + order_in_bucket(goal * size + zs, size)
+    home, hs, zr, counts, first = listed(tags[:, 128:], size)
+    came = jnp.bitwise_xor(turned(lax.shift_right_logical(zr, shift), peers), me)
+    position = order_in_bucket(came * size + jnp.bitwise_and(zr, size - 1), size * peers)
+    came_from = came == lax.broadcasted_iota(i32, (peers, size), 0)
+    counts = jnp.sum(jnp.where(came_from, 1.0, 0.0), axis=1, keepdims=True).astype(i32)
+    counts = jnp.broadcast_to(counts, (peers, 128))
+    place2_ref[...] = positions_of_slots(counts, offsets(counts), capacity, slots)
+    target = home * capacity + order_in_bucket(home * size + hs, size)
+    parts = digits((target, 2))
     for start in range(0, size, 256):
-        z_pieces.append(contract_last(z_parts, chosen(z_place, 0, start, 256, slots)))
-        h_pieces.append(contract_last(h_parts, chosen(h_place, 0, start, 256, slots)))
-    z_rows = jnp.concatenate(z_pieces, axis=1)
-    h_rows = jnp.concatenate(h_pieces, axis=1)
-    row = lax.broadcasted_iota(i32, (1, size), 1)
-    owner = lax.shift_right_logical(undigits(z_rows, 0, 3), shift)
-    target2_ref[...] = owner * capacity + order_in_bucket(owner * size + row, size)
-    zr = undigits(h_rows, 0, 3)
-    source2_ref[...] = lax.shift_right_logical(zr, shift) * capacity + order_in_bucket(zr, size)
-    home = undigits(h_rows, 3, 1)
-    target3_ref[...] = home * capacity + order_in_bucket(home * size + row, size)
-
-
-def pack_rows(target, rows, out_ref):
-    slots = out_ref.shape[0]
+        picked = contract_last(parts, chosen(position, 0, start, 256, size))
+        target3_ref[:, start : start + 256] = undigits(picked, 0, 2)
+
+
+def pack_rows(target_ref, rows_ref, packed_ref, part_refs, sem):
+    slots = packed_ref.shape[0]
+    capacity = slots // len(part_refs)
+    blocks = slots // 256
 
     def step(i, carry):
         start = pl.multiple_of(i * 256, 256)
-        pick = chosen(target, 0, start, 256, rows.shape[0])
-        out_ref[pl.ds(start, 256), :] = jnp.dot(
-            pick, rows, preferred_element_type=f32
+        pick = chosen(target_ref[...], 0, start, 256, rows_ref.shape[0])
+        packed_ref[pl.ds(start, 256), :] = jnp.dot(
+            pick, rows_ref[...], preferred_element_type=f32
         ).astype(bf16)
         return carry
 
-    lax.fori_loop(0, slots // 256, step, 0, unroll=2)
-
-
-def pack_kernel(target_ref, rows_ref, out_ref):
-    pack_rows(target_ref[...], rows_ref[...], out_ref)
-
-
-def unpack_kernel(source_ref, received_ref, out_ref, tall_ref):
+    copies = []
+    done = 0
+    for end in (blocks // 2, blocks):
+        lax.fori_loop(done, end, step, 0)
+        done = end
+        while (len(copies) + 1) * capacity <= end * 256 and len(copies) < len(part_refs):
+            i = len(copies)
+            copies.append(
+                pltpu.make_async_copy(
+                    packed_ref.at[pl.ds(i * capacity, capacity)], part_refs[i], sem.at[i]
+                )
+            )
+            copies[-1].start()
+    for copy in copies:
+        copy.wait()
+
+
+def pack_kernel(target_ref, rows_ref, *rest):
+    *part_refs, packed_ref, sem = rest
+    pack_rows(target_ref, rows_ref, packed_ref, part_refs, sem)
+
+
+def load_parts(part_refs, received_ref, sem):
+    capacity = received_ref.shape[0] // len(part_refs)
+    copies = [
+        pltpu.make_async_copy(part, received_ref.at[pl.ds(i * capacity, capacity)], sem.at[i])
+        for i, part in enumerate(part_refs)
+    ]
+    for copy in copies:
+        copy.start()
+    return copies
+
+
+def unpack_kernel(source_ref, *rest):
+    *part_refs, out_ref, received_ref, tall_ref, sem = rest
+    copies = load_parts(part_refs, received_ref, sem)
     slots = received_ref.shape[0]
     tall_ref[...] = column(source_ref[...])
+    for copy in copies:
+        copy.wait()
 
     def step(i, carry):
         start = pl.multiple_of(i * 256, 256)
@@ -242,35 +357,27 @@
     return (0.5 * x) * (1.0 + lax.erf(x * 0.7071067811865476))
 
 
-def block_kernel(
-    layer, by_source, heads,
-    index_ref, target_ref, gain_in_ref, gain_feed_ref,
-    received_hbm, in_hbm, out_hbm, up_hbm, down_hbm,
-    packed_hbm,
-    received_ref, in_ref, out_ref, up_ref, down_ref, packed_ref,
-    rows_ref, q_ref, k_ref, vt_ref, mixed_ref, block_ref, tall_ref, load_sem, store_sem,
-):
+def block_kernel(layer, heads, peers, *refs):
+    place_ref, target_ref, gain_in_ref, gain_feed_ref, in_hbm, out_hbm, up_hbm, down_hbm = refs[:8]
+    part_refs, packed_refs = refs[8 : 8 + peers], refs[8 + peers : 8 + 2 * peers]
+    (
+        received_ref, in_ref, out_ref, up_ref, down_ref, packed_ref,
+        rows_ref, q_ref, k_ref, vt_ref, mixed_ref, block_ref, load_sem, part_sem, store_sem,
+    ) = refs[8 + 2 * peers :]
     slots, width = received_ref.shape
     size = rows_ref.shape[0]
     hidden = up_ref.shape[1]
     head_size = width // heads
     scale = head_size ** (-0.5) * LOG2E
+    arrivals = load_parts(part_refs, received_ref, part_sem)
     loads = [
-        pltpu.make_async_copy(source, target, load_sem.at[i])
+        pltpu.make_async_copy(source.at[layer], target, load_sem.at[i])
         for i, (source, target) in enumerate(
-            (
-                (received_hbm, received_ref),
-                (in_hbm.at[layer], in_ref),
-                (out_hbm.at[layer], out_ref),
-                (up_hbm.at[layer], up_ref),
-                (down_hbm.at[layer], down_ref),
-            )
+            ((in_hbm, in_ref), (out_hbm, out_ref), (up_hbm, up_ref), (down_hbm, down_ref))
         )
     ]
     for load in loads:
         load.start()
-    if by_source:
-        tall_ref[...] = column(index_ref[...])
     group = jnp.where(
         lax.broadcasted_iota(i32, (width, 128), 0) // head_size
         == lax.broadcasted_iota(i32, (width, 128), 1),
@@ -278,19 +385,14 @@
         0.0,
     ).astype(bf16)
     block = 256
+    for arrival in arrivals:
+        arrival.wait()
     loads[0].wait()
-    loads[1].wait()
 
     def project(i, carry):
         q_most, k_most = carry
         start = pl.multiple_of(i * block, block)
-        if by_source:
-            tall = tall_ref[pl.ds(start, block), :]
-            pick = jnp.concatenate(
-                [chosen(tall, 1, piece, block, 128) for piece in range(0, slots, 128)], axis=1
-            )
-        else:
-            pick = chosen(index_ref[...], 0, start, block, slots)
+        pick = chosen(place_ref[...], 0, start, block, slots)
         rows = jnp.dot(pick, received_ref[...], preferred_element_type=f32).astype(bf16)
         rows_ref[pl.ds(start, block), :] = rows
         normed = normalize(rows, gain_in_ref[...])
@@ -312,7 +414,7 @@
     q_most, k_most = lax.fori_loop(0, size // block, project, (zero, zero), unroll=2)
     small = jnp.max(q_most * k_most) <= SAFE_EXPONENT * SAFE_EXPONENT
     attend(heads, small, q_ref, k_ref, vt_ref, mixed_ref)
-    for load in loads[2:]:
+    for load in loads[1:]:
         load.wait()
     piece = 512
 
@@ -336,36 +438,30 @@
         return carry
 
     lax.fori_loop(0, size // block, feed, 0, unroll=2)
-    stores = []
-    for i, start in enumerate(range(0, slots, 256)):
-        pick = chosen(target_ref[...], 0, start, 256, size)
-        packed_ref[start : start + 256, :] = jnp.dot(
-            pick, block_ref[...], preferred_element_type=f32
-        ).astype(bf16)
-        stores.append(
-            pltpu.make_async_copy(
-                packed_ref.at[pl.ds(start, 256)], packed_hbm.at[pl.ds(start, 256)], store_sem.at[i]
-            )
-        )
-        stores[-1].start()
-    for store in stores:
-        store.wait()
-
-
-def run_block(layer, by_source, index, target, received, gains_in, w_in, w_out, gains_feed, up, down):
-    slots, width = received.shape
+    pack_rows(target_ref, block_ref, packed_ref, packed_refs, store_sem)
+
+
+def parts_shape(slots, count, width):
+    return [jax.ShapeDtypeStruct((slots // count, width), bf16)] * count
+
+
+def run_block(layer, place, target, parts, gains_in, w_in, w_out, gains_feed, up, down):
+    count = len(parts)
+    width = parts[0].shape[1]
+    slots = count * parts[0].shape[0]
     size = target.shape[1]
     hidden = up.shape[2]
     vmem = pl.BlockSpec(memory_space=pltpu.VMEM)
     hbm = pl.BlockSpec(memory_space=pl.ANY)
     half = pltpu.VMEM((size, width), bf16)
+    flipped = pltpu.VMEM((width, size), bf16)
     flops = 4 * slots * size * width + size * width * (8 * width + 4 * hidden + 16 * size)
     return pl.pallas_call(
-        functools.partial(block_kernel, layer, by_source, HEADS),
+        functools.partial(block_kernel, layer, HEADS, count),
         name="block",
-        out_shape=jax.ShapeDtypeStruct((slots, width), bf16),
-        in_specs=[vmem] * 4 + [hbm] * 5,
-        out_specs=hbm,
+        out_shape=parts_shape(slots, count, width),
+        in_specs=[vmem] * 4 + [hbm] * (4 + count),
+        out_specs=[hbm] * count,
         scratch_shapes=[
             pltpu.VMEM((slots, width), bf16),
             pltpu.VMEM((width, 3 * width), bf16),
@@ -376,29 +472,40 @@
             half,
             half,
             half,
-            pltpu.VMEM((width, size), bf16),
-            pltpu.VMEM((width, size), bf16),
+            flipped,
+            flipped,
             half,
-            pltpu.VMEM((size, 128), i32),
-            pltpu.SemaphoreType.DMA((5,)),
-            pltpu.SemaphoreType.DMA((slots // 256,)),
+            pltpu.SemaphoreType.DMA((4,)),
+            pltpu.SemaphoreType.DMA((count,)),
+            pltpu.SemaphoreType.DMA((count,)),
         ],
-        compiler_params=pltpu.CompilerParams(vmem_limit_bytes=56 << 20),
+        compiler_params=pltpu.CompilerParams(vmem_limit_bytes=48 << 20),
         cost_estimate=pl.CostEstimate(
             flops=flops, bytes_accessed=4 * slots * width, transcendentals=0
         ),
     )(
-        index, target, gains_in[layer].reshape(1, width), gains_feed[layer].reshape(1, width),
-        received, w_in, w_out, up, down,
+        place, target, gains_in[layer].reshape(1, width), gains_feed[layer].reshape(1, width),
+        w_in, w_out, up, down, *parts,
     )
 
 
-def exchange(packed, peers):
-    slots, width = packed.shape
-    received = lax.all_to_all(
-        packed.reshape(peers, slots // peers, width), AXES, split_axis=0, concat_axis=0, tiled=True
-    )
-    return received.reshape(slots, width)
+def exchange(parts, peers):
+    if len(parts) == peers:
+        out = []
+        for t, part in enumerate(parts):
+            step = turned_back(t, peers)
+            out.append(
+                lax.ppermute(part, AXES, [(d, d ^ step) for d in range(peers)]) if t else part
+            )
+        return out
+    (part,) = parts
+    device = jnp.arange(peers, dtype=i32)
+    me = my_index()
+    stacked = part.reshape(peers, part.shape[0] // peers, part.shape[1])
+    stacked = jnp.take(stacked, jnp.bitwise_xor(turned(device, peers), turned(me, peers)), axis=0)
+    received = lax.all_to_all(stacked, AXES, split_axis=0, concat_axis=0, tiled=True)
+    received = jnp.take(received, jnp.bitwise_xor(turned_back(device, peers), me), axis=0)
+    return [received.reshape(part.shape)]
 
 
 def body(
@@ -409,41 +516,61 @@
     peers = lax.axis_size("gx") * lax.axis_size("gy")
     capacity = 5 * size // (2 * peers)
     slots = peers * capacity
+    count = peers if peers <= 64 and capacity % 16 == 0 else 1
 
     def shape(rows, columns, dtype):
         return jax.ShapeDtypeStruct((rows, columns), dtype)
 
     index = shape(1, size, i32)
-    tags = shape(1, slots, i32)
-    sent = shape(peers, 128, i32)
-    z_tags, h_tags, target1, source3 = call(
-        functools.partial(send_tags_kernel, size, capacity), "send_tags", (sent, sent, index, index)
+    places = shape(1, slots, i32)
+    tags, target1, source3 = call(
+        functools.partial(send_tags_kernel, size, capacity),
+        "send_tags",
+        (shape(peers, 256, i32), index, index),
     )(zorder_rank.reshape(1, size), hilbert_rank.reshape(1, size))
-    both = jnp.concatenate([z_tags, h_tags], axis=1).reshape(peers, 1, 256)
-    both = lax.all_to_all(both, AXES, split_axis=0, concat_axis=0, tiled=True)
-    z_tags = both[:, 0, :capacity].reshape(1, slots)
-    h_tags = both[:, 0, 128 : 128 + capacity].reshape(1, slots)
+    tags = lax.all_to_all(
+        tags.reshape(peers, 1, 256), AXES, split_axis=0, concat_axis=0, tiled=True
+    )
+    tags = tags.reshape(2, peers // 2, 256).transpose(1, 0, 2).reshape(peers, 256)
     select = 2 * slots * size * width
-    packed = call(pack_kernel, "pack", shape(slots, width, bf16), flops=select)(target1, features)
+    vmem = pl.BlockSpec(memory_space=pltpu.VMEM)
+    hbm = pl.BlockSpec(memory_space=pl.ANY)
+    packed = pl.pallas_call(
+        pack_kernel,
+        name="pack",
+        out_shape=parts_shape(slots, count, width),
+        in_specs=[vmem, vmem],
+        out_specs=[hbm] * count,
+        scratch_shapes=[pltpu.VMEM((slots, width), bf16), pltpu.SemaphoreType.DMA((count,))],
+        compiler_params=pltpu.CompilerParams(vmem_limit_bytes=32 << 20),
+        cost_estimate=pl.CostEstimate(flops=select, bytes_accessed=0, transcendentals=0),
+    )(target1, features)
     received = exchange(packed, peers)
-    place1, target2, source2, target3 = call(
-        functools.partial(route_kernel, size, capacity), "route", (tags, index, index, index)
-    )(z_tags, h_tags)
-
-    for layer, incoming, outgoing in ((0, place1, target2), (1, source2, target3)):
+    place1, target2, place2, target3 = call(
+        functools.partial(route_kernel, size, capacity), "route", (places, index, places, index)
+    )(tags)
+
+    for layer, place, target in ((0, place1, target2), (1, place2, target3)):
         packed = run_block(
-            layer, layer == 1, incoming, outgoing, received, attention_gain, attention_in,
+            layer, place, target, received, attention_gain, attention_in,
             attention_out, feedforward_gain, feedforward_up, feedforward_down,
         )
         received = exchange(packed, peers)
 
-    return call(
+    return pl.pallas_call(
         unpack_kernel,
-        "unpack",
-        shape(size, width, bf16),
-        scratch=[pltpu.VMEM((size, 128), i32)],
-        flops=select,
-    )(source3, received)
+        name="unpack",
+        out_shape=shape(size, width, bf16),
+        in_specs=[vmem] + [hbm] * count,
+        out_specs=vmem,
+        scratch_shapes=[
+            pltpu.VMEM((slots, width), bf16),
+            pltpu.VMEM((size, 128), i32),
+            pltpu.SemaphoreType.DMA((count,)),
+        ],
+        compiler_params=pltpu.CompilerParams(vmem_limit_bytes=32 << 20),
+        cost_estimate=pl.CostEstimate(flops=select, bytes_accessed=0, transcendentals=0),
+    )(source3, *received)
 
 
 def solution(mesh):

time: 451 us -> 464 us (1.029)
  starting transfers between devices: 12.3 us -> 146 us
  blocking collectives: 129 us -> 0 us
  Pallas kernels: 251 us -> 270 us
  waiting for transfers between devices: 52.8 us -> 41.3 us
    ppermute x0 -> x93, starting transfers between devices: none -> 141 us  [exchange(): lax.ppermute(part, AXES, [(d, d ^ step) for d in range(peers)])]
    all_to_all x2 -> x0, blocking collectives: 129 us -> none  [exchange(): lax.all_to_all(packed.reshape(peers, slots // peers, width), AXES, split_...]
    all_to_all x2 -> x1, waiting for transfers between devices: 52.8 us -> 0.01 us  [body(): lax.all_to_all(tags.reshape(peers, 1, 256), AXES, split_axis=0, concat_ax...]
    ppermute x0 -> x93, waiting for transfers between devices: none -> 41.3 us  [exchange(): lax.ppermute(part, AXES, [(d, d ^ step) for d in range(peers)])]
    pallas_call x2 -> x4, Pallas kernels: 229 us -> 261 us  [the longest x2 245 us: run_block(): pl.pallas_call(functools.partial(block_kernel, layer, HEADS, count), name...]
    pallas_call x4 -> x2, Pallas kernels: 21.5 us -> 8.26 us  [run(): pl.pallas_call(kernel, name=name, out_shape=out_shape, in_specs=[vmem] *...]
    all_to_all x2 -> x1, starting transfers between devices: 12.3 us -> 5.16 us  [body(): lax.all_to_all(tags.reshape(peers, 1, 256), AXES, split_axis=0, concat_ax...]
  transfers between devices with their start and end apart: 2 -> 94, of which waited for: 2 -> 26; matrix products, arithmetic and copies ran while one was open for 0% -> 0% of each run, Pallas kernels for 3% -> 1%
where the time goes in v3:
time: 464 us; the launch traced here: 462 us
  Pallas kernels  270 us (58%)
  starting transfers between devices  146 us (31%)
  waiting for transfers between devices  41.3 us (9%)
    pallas_call x2, Pallas kernels, run_block(): pl.pallas_call(functools.partial(block_kernel, layer, HEADS, count), name...  245 us
    ppermute x93, starting transfers between devices, exchange(): lax.ppermute(part, AXES, [(d, d ^ step) for d in range(peers)])  141 us
    ppermute x93, waiting for transfers between devices, exchange(): lax.ppermute(part, AXES, [(d, d ^ step) for d in range(peers)])  41.3 us
  transfers between devices with their start and end apart: 94, of which 26 were waited for; matrix products, arithmetic and copies ran while one was open for 0% of the time, Pallas kernels for 1%

profile of v3, /device:TPU:0, one launch (start us, length us, event | category | flops | bytes accessed | tf_op | source)
XLA Modules:
  0.0 462.2 jit_solution(6291522631821776535)
XLA Ops:
  0.0 3.2 send_tags.1
  5.1 8.5 %pack.1 = (bf16[80,512]{1,0:T(8,128)(2,1)S(1)}, bf16[80,512]{1,0:T(8,128)(2,1)S(1)}, bf16[80,512]{1,0:T(8,128)(2,1)S(1)}, bf16[80,512]{1,0:T(8,128)(2,1)S(1)}, b...) custom-call(s32[1,1024]{1,0:T(1,128)S(1)} %copy-done.6, ...), custom_call_target="tpu_custom_call" | custom-call | flops 2684354560 | tf_op jit(solution)/shard_map/pack/pallas_call | solution.py:538
  13.5 4.1 collective-permute-start
  19.6 2.5 collective-permute-start.4
  32.4 2.5 collective-permute-start.11
  40.2 6.0 %collective-permute-start.15 = (bf16[80,512]{1,0:T(8,128)(2,1)S(1)}, bf16[80,512]{1,0:T(8,128)(2,1)S(1)}, u32[]{:S(2)}, u32[]{:S(2)}) collective-permute-start(bf16[80,512]{1,0:T(8,128)(2,1)S(1)} %get-tuple-element.131), channel_id=1, source_target_pairs={{0,8},{1,9},{2,10},{3,11},{4,12},{5,13},{6,14},{7,15},{8,0},{9,1},... | collective-permute-start | bytes 245768 | tf_op jit(solution)/shard_map/ppermute | solution.py:498
  47.6 2.9 collective-permute-start.18
  52.6 2.9 collective-permute-start.20
  58.9 3.1 collective-permute-start.24
  62.7 5.2 %all-to-all-start = ((s32[32,1,256]{2,1,0:T(1,128)}), s32[32,1,256]{2,1,0:T(1,128)S(1)}, u32[]{:S(2)}, u32[]{:S(2)}) async-start(s32[32,1,256]{2,1,0:T(1,128)} %copy.11), calls=%async_computation | async-start | bytes 65536 | tf_op jit(solution)/shard_map/all_to_all | solution.py:531
  67.9 4.2 collective-permute-start.26
  75.8 4.5 collective-permute-start.30
  81.0 5.1 %route.1 = (s32[1,2560]{1,0:T(1,128)}, s32[1,1024]{1,0:T(1,128)}, s32[1,2560]{1,0:T(1,128)}, s32[1,1024]{1,0:T(1,128)}) custom-call(s32[32,256]{1,0:T(8,128)} %reshape.19.tag_ref), custom_call_target="tpu_custom_call" | custom-call | bytes 32768 | tf_op jit(solution)/shard_map/route/pallas_call | solution.py:27
  87.5 122.2 %block.2 = (bf16[80,512]{1,0:T(8,128)(2,1)S(1)}, bf16[80,512]{1,0:T(8,128)(2,1)S(1)}, bf16[80,512]{1,0:T(8,128)(2,1)S(1)}, bf16[80,512]{1,0:T(8,128)(2,1)S(1)}, ...) custom-call(s32[1,2560]{1,0:T(1,128)S(1)} %copy-done.2, ...), custom_call_target="tpu_custom_call" | custom-call | flops 20401094656 | bytes 5242880 | tf_op jit(solution)/shard_map/block/pallas_call | solution.py:459
  210.2 2.7 collective-permute-start.33
  214.4 6.3 %collective-permute-done.31.refs_9_ = bf16[80,512]{1,0:T(8,128)(2,1)S(1)} collective-permute-done((bf16[80,512]{1,0:T(8,128)(2,1)S(1)}, bf16[80,512]{1,0:T(8,128)(2,1)S(1)}, u32[]{:S(2)}, u32[]{:S(2)}) %collective-permute-start.31) | collective-permute-done | bytes 81952 | tf_op jit(solution)/shard_map/ppermute | solution.py:498
  222.6 3.7 collective-permute-start.39
  228.7 4.1 collective-permute-start.43
  250.9 4.0 collective-permute-start.55
  254.9 3.2 collective-permute-start.57
  259.6 2.6 collective-permute-start.59
  262.7 4.4 collective-permute-start.61
  272.1 122.4 %block.3 = (bf16[80,512]{1,0:T(8,128)(2,1)S(1)}, bf16[80,512]{1,0:T(8,128)(2,1)S(1)}, bf16[80,512]{1,0:T(8,128)(2,1)S(1)}, bf16[80,512]{1,0:T(8,128)(2,1)S(1)}, ...) custom-call(s32[1,2560]{1,0:T(1,128)S(1)} %copy-done.1, ...), custom_call_target="tpu_custom_call" | custom-call | flops 20401094656 | bytes 5242880 | tf_op jit(solution)/shard_map/block/pallas_call | solution.py:459
  397.6 3.1 collective-permute-start.66
  400.7 3.9 collective-permute-done.62.rest_1_
  406.3 3.8 collective-permute-start.70
  413.5 3.1 collective-permute-start.74
  419.6 2.7 collective-permute-start.77
  434.1 3.3 collective-permute-done.81.rest_20_
  442.1 3.3 collective-permute-start.90
  445.5 4.3 collective-permute-start.92
  453.8 8.2 %unpack.1 = bf16[1024,512]{1,0:T(8,128)(2,1)} custom-call(s32[1,1024]{1,0:T(1,128)S(1)} %copy-done.3, bf16[80,512]{1,0:T(8,128)(2,1)S(1)} %get-tuple-element.179.rest_0_, bf16[80,512]{1,0:T(8,128)(2,1)S(1)} %collective-permute-done.62.rest_1_, bf16[80,512]{1,0:T(8,128)(2,1)S(1)} %collective-permute-done.63.rest_2_, ...), custom_call_target="tpu_custom_call" | custom-call | flops 2684354560 | tf_op jit(solution)/shard_map/unpack/pallas_call | solution.py:560
  (187 shorter events, 95.9 us)
Async XLA Ops:
  17.9 10.5 %collective-permute-start.3 = (bf16[80,512]{1,0:T(8,128)(2,1)S(1)}, bf16[80,512]{1,0:T(8,128)(2,1)S(1)}, u32[]{:S(2)}, u32[]{:S(2)}) collective-permute-start(bf16[80,512]{1,0:T(8,128)(2,1)S(1)} %get-tuple-element.119), channel_id=1, source_target_pairs={{0,2},{1,3},{2,0},{3,1},{4,6},{5,7},{6,4},{7,5},{8,10},{9,11},{10,... | collective-permute-start | bytes 245768 | tf_op jit(solution)/shard_map/ppermute | solution.py:498
  19.6 10.9 %collective-permute-start.4 = (bf16[80,512]{1,0:T(8,128)(2,1)S(1)}, bf16[80,512]{1,0:T(8,128)(2,1)S(1)}, u32[]{:S(2)}, u32[]{:S(2)}) collective-permute-start(bf16[80,512]{1,0:T(8,128)(2,1)S(1)} %get-tuple-element.120), channel_id=1, source_target_pairs={{0,18},{1,19},{2,16},{3,17},{4,22},{5,23},{6,20},{7,21},{8,26},{9,... | collective-permute-start | bytes 245768 | tf_op jit(solution)/shard_map/ppermute | solution.py:498
  28.3 10.4 %collective-permute-start.8 = (bf16[80,512]{1,0:T(8,128)(2,1)S(1)}, bf16[80,512]{1,0:T(8,128)(2,1)S(1)}, u32[]{:S(2)}, u32[]{:S(2)}) collective-permute-start(bf16[80,512]{1,0:T(8,128)(2,1)S(1)} %get-tuple-element.124), channel_id=1, source_target_pairs={{0,20},{1,21},{2,22},{3,23},{4,16},{5,17},{6,18},{7,19},{8,28},{9,... | collective-permute-start | bytes 245768 | tf_op jit(solution)/shard_map/ppermute | solution.py:498
  32.4 13.8 %collective-permute-start.11 = (bf16[80,512]{1,0:T(8,128)(2,1)S(1)}, bf16[80,512]{1,0:T(8,128)(2,1)S(1)}, u32[]{:S(2)}, u32[]{:S(2)}) collective-permute-start(bf16[80,512]{1,0:T(8,128)(2,1)S(1)} %get-tuple-element.127), channel_id=1, source_target_pairs={{0,6},{1,7},{2,4},{3,5},{4,2},{5,3},{6,0},{7,1},{8,14},{9,15},{10,... | collective-permute-start | bytes 245768 | tf_op jit(solution)/shard_map/ppermute | solution.py:498
  34.9 12.1 %collective-permute-start.12 = (bf16[80,512]{1,0:T(8,128)(2,1)S(1)}, bf16[80,512]{1,0:T(8,128)(2,1)S(1)}, u32[]{:S(2)}, u32[]{:S(2)}) collective-permute-start(bf16[80,512]{1,0:T(8,128)(2,1)S(1)} %get-tuple-element.128), channel_id=1, source_target_pairs={{0,22},{1,23},{2,20},{3,21},{4,18},{5,19},{6,16},{7,17},{8,30},{9,... | collective-permute-start | bytes 245768 | tf_op jit(solution)/shard_map/ppermute | solution.py:498
  38.8 11.7 %collective-permute-start.14 = (bf16[80,512]{1,0:T(8,128)(2,1)S(1)}, bf16[80,512]{1,0:T(8,128)(2,1)S(1)}, u32[]{:S(2)}, u32[]{:S(2)}) collective-permute-start(bf16[80,512]{1,0:T(8,128)(2,1)S(1)} %get-tuple-element.130), channel_id=1, source_target_pairs={{0,23},{1,22},{2,21},{3,20},{4,19},{5,18},{6,17},{7,16},{8,31},{9,... | collective-permute-start | bytes 245768 | tf_op jit(solution)/shard_map/ppermute | solution.py:498
  40.2 12.4 %collective-permute-start.15 = (bf16[80,512]{1,0:T(8,128)(2,1)S(1)}, bf16[80,512]{1,0:T(8,128)(2,1)S(1)}, u32[]{:S(2)}, u32[]{:S(2)}) collective-permute-start(bf16[80,512]{1,0:T(8,128)(2,1)S(1)} %get-tuple-element.131), channel_id=1, source_target_pairs={{0,8},{1,9},{2,10},{3,11},{4,12},{5,13},{6,14},{7,15},{8,0},{9,1},... | collective-permute-start | bytes 245768 | tf_op jit(solution)/shard_map/ppermute | solution.py:498
  55.5 12.3 %collective-permute-start.21 = (bf16[80,512]{1,0:T(8,128)(2,1)S(1)}, bf16[80,512]{1,0:T(8,128)(2,1)S(1)}, u32[]{:S(2)}, u32[]{:S(2)}) collective-permute-start(bf16[80,512]{1,0:T(8,128)(2,1)S(1)} %get-tuple-element.137), channel_id=1, source_target_pairs={{0,11},{1,10},{2,9},{3,8},{4,15},{5,14},{6,13},{7,12},{8,3},{9,2},... | collective-permute-start | bytes 245768 | tf_op jit(solution)/shard_map/ppermute | solution.py:498
  55.5 16.5 %collective-permute-start.22 = (bf16[80,512]{1,0:T(8,128)(2,1)S(1)}, bf16[80,512]{1,0:T(8,128)(2,1)S(1)}, u32[]{:S(2)}, u32[]{:S(2)}) collective-permute-start(bf16[80,512]{1,0:T(8,128)(2,1)S(1)} %get-tuple-element.138), channel_id=1, source_target_pairs={{0,27},{1,26},{2,25},{3,24},{4,31},{5,30},{6,29},{7,28},{8,19},{9,... | collective-permute-start | bytes 245768 | tf_op jit(solution)/shard_map/ppermute | solution.py:498
  57.4 15.1 %collective-permute-start.23 = (bf16[80,512]{1,0:T(8,128)(2,1)S(1)}, bf16[80,512]{1,0:T(8,128)(2,1)S(1)}, u32[]{:S(2)}, u32[]{:S(2)}) collective-permute-start(bf16[80,512]{1,0:T(8,128)(2,1)S(1)} %get-tuple-element.139), channel_id=1, source_target_pairs={{0,12},{1,13},{2,14},{3,15},{4,8},{5,9},{6,10},{7,11},{8,4},{9,5},... | collective-permute-start | bytes 245768 | tf_op jit(solution)/shard_map/ppermute | solution.py:498
  58.9 16.0 %collective-permute-start.24 = (bf16[80,512]{1,0:T(8,128)(2,1)S(1)}, bf16[80,512]{1,0:T(8,128)(2,1)S(1)}, u32[]{:S(2)}, u32[]{:S(2)}) collective-permute-start(bf16[80,512]{1,0:T(8,128)(2,1)S(1)} %get-tuple-element.140), channel_id=1, source_target_pairs={{0,28},{1,29},{2,30},{3,31},{4,24},{5,25},{6,26},{7,27},{8,20},{9,... | collective-permute-start | bytes 245768 | tf_op jit(solution)/shard_map/ppermute | solution.py:498
  62.0 13.8 %collective-permute-start.25 = (bf16[80,512]{1,0:T(8,128)(2,1)S(1)}, bf16[80,512]{1,0:T(8,128)(2,1)S(1)}, u32[]{:S(2)}, u32[]{:S(2)}) collective-permute-start(bf16[80,512]{1,0:T(8,128)(2,1)S(1)} %get-tuple-element.141), channel_id=1, source_target_pairs={{0,13},{1,12},{2,15},{3,14},{4,9},{5,8},{6,11},{7,10},{8,5},{9,4},... | collective-permute-start | bytes 245768 | tf_op jit(solution)/shard_map/ppermute | solution.py:498
  62.7 17.6 %all-to-all-start = ((s32[32,1,256]{2,1,0:T(1,128)}), s32[32,1,256]{2,1,0:T(1,128)S(1)}, u32[]{:S(2)}, u32[]{:S(2)}) async-start(s32[32,1,256]{2,1,0:T(1,128)} %copy.11), calls=%async_computation | async-start | bytes 65536 | tf_op jit(solution)/shard_map/all_to_all | solution.py:531
  67.9 18.3 %collective-permute-start.26 = (bf16[80,512]{1,0:T(8,128)(2,1)S(1)}, bf16[80,512]{1,0:T(8,128)(2,1)S(1)}, u32[]{:S(2)}, u32[]{:S(2)}) collective-permute-start(bf16[80,512]{1,0:T(8,128)(2,1)S(1)} %get-tuple-element.142), channel_id=1, source_target_pairs={{0,29},{1,28},{2,31},{3,30},{4,25},{5,24},{6,27},{7,26},{8,21},{9,... | collective-permute-start | bytes 245768 | tf_op jit(solution)/shard_map/ppermute | solution.py:498
  72.0 14.1 %collective-permute-start.27 = (bf16[80,512]{1,0:T(8,128)(2,1)S(1)}, bf16[80,512]{1,0:T(8,128)(2,1)S(1)}, u32[]{:S(2)}, u32[]{:S(2)}) collective-permute-start(bf16[80,512]{1,0:T(8,128)(2,1)S(1)} %get-tuple-element.143), channel_id=1, source_target_pairs={{0,14},{1,15},{2,12},{3,13},{4,10},{5,11},{6,8},{7,9},{8,6},{9,7},... | collective-permute-start | bytes 245768 | tf_op jit(solution)/shard_map/ppermute | solution.py:498
  72.5 13.6 %collective-permute-start.28 = (bf16[80,512]{1,0:T(8,128)(2,1)S(1)}, bf16[80,512]{1,0:T(8,128)(2,1)S(1)}, u32[]{:S(2)}, u32[]{:S(2)}) collective-permute-start(bf16[80,512]{1,0:T(8,128)(2,1)S(1)} %get-tuple-element.144), channel_id=1, source_target_pairs={{0,30},{1,31},{2,28},{3,29},{4,26},{5,27},{6,24},{7,25},{8,22},{9,... | collective-permute-start | bytes 245768 | tf_op jit(solution)/shard_map/ppermute | solution.py:498
  74.9 11.3 %collective-permute-start.29 = (bf16[80,512]{1,0:T(8,128)(2,1)S(1)}, bf16[80,512]{1,0:T(8,128)(2,1)S(1)}, u32[]{:S(2)}, u32[]{:S(2)}) collective-permute-start(bf16[80,512]{1,0:T(8,128)(2,1)S(1)} %get-tuple-element.145), channel_id=1, source_target_pairs={{0,15},{1,14},{2,13},{3,12},{4,11},{5,10},{6,9},{7,8},{8,7},{9,6},... | collective-permute-start | bytes 245768 | tf_op jit(solution)/shard_map/ppermute | solution.py:498
  209.8 10.9 %collective-permute-start.31 = (bf16[80,512]{1,0:T(8,128)(2,1)S(1)}, bf16[80,512]{1,0:T(8,128)(2,1)S(1)}, u32[]{:S(2)}, u32[]{:S(2)}) collective-permute-start(bf16[80,512]{1,0:T(8,128)(2,1)S(1)} %get-tuple-element.148), channel_id=1, source_target_pairs={{0,16},{1,17},{2,18},{3,19},{4,20},{5,21},{6,22},{7,23},{8,24},{9,... | collective-permute-start | bytes 245768 | tf_op jit(solution)/shard_map/ppermute | solution.py:498
  209.9 11.1 %collective-permute-start.32 = (bf16[80,512]{1,0:T(8,128)(2,1)S(1)}, bf16[80,512]{1,0:T(8,128)(2,1)S(1)}, u32[]{:S(2)}, u32[]{:S(2)}) collective-permute-start(bf16[80,512]{1,0:T(8,128)(2,1)S(1)} %get-tuple-element.149), channel_id=1, source_target_pairs={{0,1},{1,0},{2,3},{3,2},{4,5},{5,4},{6,7},{7,6},{8,9},{9,8},{10,11... | collective-permute-start | bytes 245768 | tf_op jit(solution)/shard_map/ppermute | solution.py:498
  210.2 11.3 %collective-permute-start.33 = (bf16[80,512]{1,0:T(8,128)(2,1)S(1)}, bf16[80,512]{1,0:T(8,128)(2,1)S(1)}, u32[]{:S(2)}, u32[]{:S(2)}) collective-permute-start(bf16[80,512]{1,0:T(8,128)(2,1)S(1)} %get-tuple-element.150), channel_id=1, source_target_pairs={{0,17},{1,16},{2,19},{3,18},{4,21},{5,20},{6,23},{7,22},{8,25},{9,... | collective-permute-start | bytes 245768 | tf_op jit(solution)/shard_map/ppermute | solution.py:498
  214.4 11.9 %collective-permute-start.35 = (bf16[80,512]{1,0:T(8,128)(2,1)S(1)}, bf16[80,512]{1,0:T(8,128)(2,1)S(1)}, u32[]{:S(2)}, u32[]{:S(2)}) collective-permute-start(bf16[80,512]{1,0:T(8,128)(2,1)S(1)} %get-tuple-element.152), channel_id=1, source_target_pairs={{0,18},{1,19},{2,16},{3,17},{4,22},{5,23},{6,20},{7,21},{8,26},{9,... | collective-permute-start | bytes 245768 | tf_op jit(solution)/shard_map/ppermute | solution.py:498
  222.6 11.0 %collective-permute-start.39 = (bf16[80,512]{1,0:T(8,128)(2,1)S(1)}, bf16[80,512]{1,0:T(8,128)(2,1)S(1)}, u32[]{:S(2)}, u32[]{:S(2)}) collective-permute-start(bf16[80,512]{1,0:T(8,128)(2,1)S(1)} %get-tuple-element.156), channel_id=1, source_target_pairs={{0,20},{1,21},{2,22},{3,23},{4,16},{5,17},{6,18},{7,19},{8,28},{9,... | collective-permute-start | bytes 245768 | tf_op jit(solution)/shard_map/ppermute | solution.py:498
  227.5 11.1 %collective-permute-start.42 = (bf16[80,512]{1,0:T(8,128)(2,1)S(1)}, bf16[80,512]{1,0:T(8,128)(2,1)S(1)}, u32[]{:S(2)}, u32[]{:S(2)}) collective-permute-start(bf16[80,512]{1,0:T(8,128)(2,1)S(1)} %get-tuple-element.159), channel_id=1, source_target_pairs={{0,6},{1,7},{2,4},{3,5},{4,2},{5,3},{6,0},{7,1},{8,14},{9,15},{10,... | collective-permute-start | bytes 245768 | tf_op jit(solution)/shard_map/ppermute | solution.py:498
  228.7 11.5 %collective-permute-start.43 = (bf16[80,512]{1,0:T(8,128)(2,1)S(1)}, bf16[80,512]{1,0:T(8,128)(2,1)S(1)}, u32[]{:S(2)}, u32[]{:S(2)}) collective-permute-start(bf16[80,512]{1,0:T(8,128)(2,1)S(1)} %get-tuple-element.160), channel_id=1, source_target_pairs={{0,22},{1,23},{2,20},{3,21},{4,18},{5,19},{6,16},{7,17},{8,30},{9,... | collective-permute-start | bytes 245768 | tf_op jit(solution)/shard_map/ppermute | solution.py:498
  247.4 10.7 %collective-permute-start.53 = (bf16[80,512]{1,0:T(8,128)(2,1)S(1)}, bf16[80,512]{1,0:T(8,128)(2,1)S(1)}, u32[]{:S(2)}, u32[]{:S(2)}) collective-permute-start(bf16[80,512]{1,0:T(8,128)(2,1)S(1)} %get-tuple-element.170), channel_id=1, source_target_pairs={{0,27},{1,26},{2,25},{3,24},{4,31},{5,30},{6,29},{7,28},{8,19},{9,... | collective-permute-start | bytes 245768 | tf_op jit(solution)/shard_map/ppermute | solution.py:498
  250.9 11.4 %collective-permute-start.55 = (bf16[80,512]{1,0:T(8,128)(2,1)S(1)}, bf16[80,512]{1,0:T(8,128)(2,1)S(1)}, u32[]{:S(2)}, u32[]{:S(2)}) collective-permute-start(bf16[80,512]{1,0:T(8,128)(2,1)S(1)} %get-tuple-element.172), channel_id=1, source_target_pairs={{0,28},{1,29},{2,30},{3,31},{4,24},{5,25},{6,26},{7,27},{8,20},{9,... | collective-permute-start | bytes 245768 | tf_op jit(solution)/shard_map/ppermute | solution.py:498
  254.9 12.3 %collective-permute-start.57 = (bf16[80,512]{1,0:T(8,128)(2,1)S(1)}, bf16[80,512]{1,0:T(8,128)(2,1)S(1)}, u32[]{:S(2)}, u32[]{:S(2)}) collective-permute-start(bf16[80,512]{1,0:T(8,128)(2,1)S(1)} %get-tuple-element.174), channel_id=1, source_target_pairs={{0,29},{1,28},{2,31},{3,30},{4,25},{5,24},{6,27},{7,26},{8,21},{9,... | collective-permute-start | bytes 245768 | tf_op jit(solution)/shard_map/ppermute | solution.py:498
  397.6 12.6 %collective-permute-start.66 = (bf16[80,512]{1,0:T(8,128)(2,1)S(1)}, bf16[80,512]{1,0:T(8,128)(2,1)S(1)}, u32[]{:S(2)}, u32[]{:S(2)}) collective-permute-start(bf16[80,512]{1,0:T(8,128)(2,1)S(1)} %get-tuple-element.184), channel_id=1, source_target_pairs={{0,18},{1,19},{2,16},{3,17},{4,22},{5,23},{6,20},{7,21},{8,26},{9,... | collective-permute-start | bytes 245768 | tf_op jit(solution)/shard_map/ppermute | solution.py:498
  406.3 11.2 %collective-permute-start.70 = (bf16[80,512]{1,0:T(8,128)(2,1)S(1)}, bf16[80,512]{1,0:T(8,128)(2,1)S(1)}, u32[]{:S(2)}, u32[]{:S(2)}) collective-permute-start(bf16[80,512]{1,0:T(8,128)(2,1)S(1)} %get-tuple-element.188), channel_id=1, source_target_pairs={{0,20},{1,21},{2,22},{3,23},{4,16},{5,17},{6,18},{7,19},{8,28},{9,... | collective-permute-start | bytes 245768 | tf_op jit(solution)/shard_map/ppermute | solution.py:498
  413.5 10.5 %collective-permute-start.74 = (bf16[80,512]{1,0:T(8,128)(2,1)S(1)}, bf16[80,512]{1,0:T(8,128)(2,1)S(1)}, u32[]{:S(2)}, u32[]{:S(2)}) collective-permute-start(bf16[80,512]{1,0:T(8,128)(2,1)S(1)} %get-tuple-element.192), channel_id=1, source_target_pairs={{0,22},{1,23},{2,20},{3,21},{4,18},{5,19},{6,16},{7,17},{8,30},{9,... | collective-permute-start | bytes 245768 | tf_op jit(solution)/shard_map/ppermute | solution.py:498
  426.7 10.7 %collective-permute-start.81 = (bf16[80,512]{1,0:T(8,128)(2,1)S(1)}, bf16[80,512]{1,0:T(8,128)(2,1)S(1)}, u32[]{:S(2)}, u32[]{:S(2)}) collective-permute-start(bf16[80,512]{1,0:T(8,128)(2,1)S(1)} %get-tuple-element.199), channel_id=1, source_target_pairs={{0,10},{1,11},{2,8},{3,9},{4,14},{5,15},{6,12},{7,13},{8,2},{9,3},... | collective-permute-start | bytes 245768 | tf_op jit(solution)/shard_map/ppermute | solution.py:498
  429.6 11.1 %collective-permute-start.83 = (bf16[80,512]{1,0:T(8,128)(2,1)S(1)}, bf16[80,512]{1,0:T(8,128)(2,1)S(1)}, u32[]{:S(2)}, u32[]{:S(2)}) collective-permute-start(bf16[80,512]{1,0:T(8,128)(2,1)S(1)} %get-tuple-element.201), channel_id=1, source_target_pairs={{0,11},{1,10},{2,9},{3,8},{4,15},{5,14},{6,13},{7,12},{8,3},{9,2},... | collective-permute-start | bytes 245768 | tf_op jit(solution)/shard_map/ppermute | solution.py:498
  (72 other events, 1286.0 us)
